TPU v7x, 256 devices: a whole 4x4x8 slice. The times are simulated.
256 devices in a mesh: seq: 64 (over z, y, core), tensor: 4 (over x).
Axes of the slice: x: 4, y: 4, z: 8, core: 2. Of those that a mesh axis runs over, the one named last changes fastest.
Arguments:
- tokens: bfloat16 [8192, 1536], P('seq', 'tensor'), may hold values from -6 to 6
- attn_gain: float32 [1536], replicated, may hold values from 0.5 to 1.5
- q_weight: bfloat16 [1536, 1536], P(None, 'tensor'), may hold values from -0.15625 to 0.15625
- key_matrix: bfloat16 [1536, 512], P(None, 'tensor'), may hold values from -0.15625 to 0.15625
- value_matrix: bfloat16 [1536, 512], P(None, 'tensor'), may hold values from -0.15625 to 0.15625
- o_weight: bfloat16 [1536, 1536], P('tensor'), may hold values from -0.625 to 0.625
- moe_gain: float32 [1536], replicated, may hold values from 0.5 to 1.5
- gate_weight: bfloat16 [64, 1536, 512], P('seq', None, 'tensor'), may hold values from -0.15625 to 0.15625
- up_weight: bfloat16 [64, 1536, 512], P('seq', None, 'tensor'), may hold values from -0.15625 to 0.15625
- down_weight: bfloat16 [64, 512, 1536], P('seq', 'tensor'), may hold values from -0.25 to 0.25
- key_page_pool: bfloat16 [4096, 128, 512], P('seq', None, 'tensor'), may hold values from -140 to 140
- value_page_pool: bfloat16 [4096, 128, 512], P('seq', None, 'tensor'), may hold values from -6 to 6
- cache_lens: int32 [64], P('seq'), may hold values from 1 to 8192, as said below
- page_table: int32 [64, 64], P('seq'), may hold values from 0 to 63, each once within a row
- routes: int32 [8192, 8], P('seq'), may hold values from 0 to 39, all different within a row; in each aligned block of 128 rows (0 to 127, 128 to 255, ...) at most 32 rows name the same one
- route_gates: float32 [8192, 8], P('seq'), may hold values from 0.1 to 1
Outputs:
- mixed: bfloat16 [8192, 1536], P('seq', 'tensor')
Inputs may be any that keep to these rules, and one draw needn't show every extreme that they name: `cache_lens`: some request has exactly 8192 cached tokens in every draw. `page_table`: each row is a permutation of 0 .. 63. `routes`: each row names 8 different experts. Among the 128 rows of one request no expert is named more than 32 times, a bound that some block reaches.
All inputs are finite; a program needn't handle non-finite values.
Results may differ from a plain program's by a relative error of at most 0.017.
The roundings to bfloat16 on the way count: a program that leaves them out, or rounds other values in their place, can miss the bound.
Values may be sent and summed in bfloat16 or wider, within the bound.
A program may use at most 128 MiB of HBM per device.

v0:
```python
import jax
import jax.numpy as jnp
from jax import lax
from jax.sharding import PartitionSpec as P

HEAD_SIZE = 64
CAP = 32


NORM_EPSILON = 1e-06
MASKED_SCORE = -1e30


def norm_rows(field, gain_row):
    widened = field.astype(jnp.float32)
    return (
        widened
        * lax.rsqrt(jnp.mean(widened * widened, axis=1, keepdims=True) + NORM_EPSILON)
        * gain_row
    )


def apply_rotary(field, token_places):
    head_dim = field.shape[-1]
    half_dim = head_dim // 2
    frequency = 10000.0 ** (-2.0 * jnp.arange(half_dim, dtype=jnp.float32) / head_dim)
    phase_angle = token_places[:, None, None] * frequency
    cosine = jnp.cos(phase_angle)
    sine_part = jnp.sin(phase_angle)
    lower_half = field[..., :half_dim]
    upper_half = field[..., half_dim:]
    return jnp.concatenate(
        [
            lower_half * cosine - upper_half * sine_part,
            upper_half * cosine + lower_half * sine_part,
        ],
        axis=-1,
    )


def attend(
    query_rows, incoming_keys, incoming_values, key_pool, value_pool, table_row, cached_length
):
    row_count = query_rows.shape[0]
    kv_count = incoming_keys.shape[1]
    head_dim = incoming_keys.shape[2]
    page_count = key_pool.shape[0]
    page_rows = key_pool.shape[1]
    per_block = min(page_count, max(1, 512 // page_rows))
    block_count = page_count // per_block
    block_span = per_block * page_rows
    score_scale = head_dim ** (-0.5)
    causal = jnp.arange(row_count)[None, :] <= jnp.arange(row_count)[:, None]
    fresh_scores = (
        jnp.einsum("tgjd,sgd->gjts", query_rows, incoming_keys, preferred_element_type=jnp.float32)
        * score_scale
    )
    fresh_scores = jnp.where(causal, fresh_scores, MASKED_SCORE)

    def load_block(pool, block_id):
        page_index = lax.dynamic_slice_in_dim(table_row, block_id * per_block, per_block)
        return pool[page_index].reshape(block_span, kv_count, head_dim)

    def weighted(scores, values, row_best):
        weights = jnp.exp(scores - row_best[..., None])
        weights_b = weights.astype(jnp.bfloat16)
        return (
            jnp.sum(weights, axis=-1),
            jnp.einsum("gjts,sgd->gjtd", weights_b, values, preferred_element_type=jnp.float32),
        )

    def block_step(block_id, carried):
        old_best, old_total, old_mix = carried
        block_keys = load_block(key_pool, block_id)
        scores = (
            jnp.einsum("tgjd,sgd->gjts", query_rows, block_keys, preferred_element_type=jnp.float32)
            * score_scale
        )
        visible = block_id * block_span + jnp.arange(block_span, dtype=jnp.int32) < cached_length
        scores = jnp.where(visible, scores, MASKED_SCORE)
        new_best = jnp.maximum(old_best, jnp.max(scores, axis=-1))
        rescale = jnp.exp(old_best - new_best)
        block_total, block_mix = weighted(scores, load_block(value_pool, block_id), new_best)
        return (
            new_best,
            old_total * rescale + block_total,
            old_mix * rescale[..., None] + block_mix,
        )

    first_best = jnp.max(fresh_scores, axis=-1)
    first_total, first_mix = weighted(fresh_scores, incoming_values, first_best)
    _, denominator, mixture = lax.fori_loop(
        0, block_count, block_step, (first_best, first_total, first_mix)
    )
    result = mixture / denominator[..., None]
    return jnp.transpose(result, (2, 0, 1, 3)).reshape(row_count, -1).astype(jnp.bfloat16)


def slot_places(routes, capacity, expert_total):
    flat_routes = routes.reshape(-1)
    route_hits = (
        flat_routes[:, None] == jnp.arange(expert_total, dtype=jnp.int32)[None, :]
    ).astype(jnp.int32)
    earlier = jnp.cumsum(route_hits, axis=0) - route_hits
    return flat_routes * capacity + jnp.sum(earlier * route_hits, axis=1)


def pack_rows(moe_in, slot_place, capacity, expert_total):
    top_count = slot_place.shape[0] // moe_in.shape[0]
    token_rows = jnp.arange(slot_place.shape[0], dtype=jnp.int32) // top_count
    outgoing = jnp.zeros((expert_total * capacity, moe_in.shape[1]), moe_in.dtype)
    outgoing = outgoing.at[slot_place].set(moe_in[token_rows])
    return outgoing.reshape(expert_total, capacity, moe_in.shape[1])


def finish_partial(gate_act, up_act, down_weight, slot_place, route_gates, residual_cols):
    row_count = residual_cols.shape[0]
    hidden = (jax.nn.silu(gate_act) * up_act).astype(jnp.bfloat16)
    expert_out = jnp.einsum(
        "secf,efd->secd", hidden, down_weight, preferred_element_type=jnp.float32
    )
    expert_cols = lax.psum_scatter(
        expert_out.astype(jnp.bfloat16), "tensor", scatter_dimension=3, tiled=True
    )
    col_count = expert_cols.shape[3]
    returned = lax.all_to_all(
        expert_cols.reshape(-1, expert_cols.shape[2], col_count),
        "seq",
        split_axis=0,
        concat_axis=0,
        tiled=True,
    )
    picked = (
        returned.reshape(-1, col_count)[slot_place].astype(jnp.float32)
        * route_gates.reshape(-1)[:, None]
    )
    expert_mix = jnp.sum(picked.reshape(row_count, -1, col_count), axis=1)
    return (residual_cols.astype(jnp.float32) + expert_mix).astype(jnp.bfloat16)


def shards(
    tokens,
    attn_gain,
    q_weight,
    key_matrix,
    value_matrix,
    o_weight,
    moe_gain,
    gate_weight,
    up_weight,
    down_weight,
    key_page_pool,
    value_page_pool,
    cache_lens,
    page_table,
    routes,
    route_gates,
):
    row_count = tokens.shape[0]
    col_count = tokens.shape[1]
    group_count = lax.axis_size("seq")
    tensor_index = lax.axis_index("tensor")
    column_start = tensor_index * col_count
    local_experts = gate_weight.shape[0]
    expert_total = local_experts * group_count
    whole = lax.all_gather(tokens, "tensor", axis=1, tiled=True)
    normed = norm_rows(whole, attn_gain).astype(jnp.bfloat16)
    head_count = q_weight.shape[1] // HEAD_SIZE
    kv_count = key_matrix.shape[1] // HEAD_SIZE
    token_places = (cache_lens[0] + jnp.arange(row_count, dtype=jnp.int32)).astype(jnp.float32)
    query_rows = jnp.dot(normed, q_weight, preferred_element_type=jnp.float32).reshape(
        row_count, head_count, HEAD_SIZE
    )
    query_rows = (
        apply_rotary(query_rows, token_places)
        .astype(jnp.bfloat16)
        .reshape(row_count, kv_count, head_count // kv_count, HEAD_SIZE)
    )
    incoming_keys = jnp.dot(normed, key_matrix, preferred_element_type=jnp.float32).reshape(
        row_count, kv_count, HEAD_SIZE
    )
    incoming_keys = apply_rotary(incoming_keys, token_places).astype(jnp.bfloat16)
    incoming_values = (
        jnp.dot(normed, value_matrix, preferred_element_type=jnp.float32)
        .reshape(row_count, kv_count, HEAD_SIZE)
        .astype(jnp.bfloat16)
    )
    attended = attend(
        query_rows,
        incoming_keys,
        incoming_values,
        key_page_pool,
        value_page_pool,
        page_table[0],
        cache_lens[0],
    )
    partial_value = jnp.dot(attended, o_weight, preferred_element_type=jnp.float32)
    slot_place = slot_places(routes, CAP, expert_total)
    summed = lax.psum(partial_value.astype(jnp.bfloat16), "tensor").astype(jnp.float32)
    residual = (whole.astype(jnp.float32) + summed).astype(jnp.bfloat16)
    moe_in = norm_rows(residual, moe_gain).astype(jnp.bfloat16)
    residual_cols = lax.dynamic_slice_in_dim(residual, column_start, col_count, 1)
    received = lax.all_to_all(
        pack_rows(moe_in, slot_place, CAP, expert_total),
        "seq",
        split_axis=0,
        concat_axis=0,
        tiled=True,
    )
    received = received.reshape(group_count, local_experts, CAP, -1)
    gate_act = jnp.einsum(
        "secd,edf->secf", received, gate_weight, preferred_element_type=jnp.float32
    )
    up_act = jnp.einsum("secd,edf->secf", received, up_weight, preferred_element_type=jnp.float32)
    return finish_partial(gate_act, up_act, down_weight, slot_place, route_gates, residual_cols)


def solution(mesh):
    in_specs = (
        P("seq", "tensor"),
        P(),
        P(None, "tensor"),
        P(None, "tensor"),
        P(None, "tensor"),
        P("tensor", None),
        P(),
        P("seq", None, "tensor"),
        P("seq", None, "tensor"),
        P("seq", "tensor", None),
        P("seq", None, "tensor"),
        P("seq", None, "tensor"),
        P("seq"),
        P("seq", None),
        P("seq", None),
        P("seq", None),
    )
    out_specs = P("seq", "tensor")
    return jax.shard_map(shards, mesh=mesh, in_specs=in_specs, out_specs=out_specs, check_vma=False)
```

profile of v0, /device:TPU:8, one launch (start us, length us, event | category | flops | bytes accessed | tf_op | source)
XLA Modules:
  0.0 581.9 jit_solution(12883326083600127530)
XLA Ops:
  6.6 13.4 %all_gather.3 = bf16[128,1536]{1,0:T(8,128)(2,1)S(1)} all-gather(bf16[128,384]{1,0:T(8,128)(2,1)} %param.18), channel_id=1, replica_groups=mesh['seq'=64,'tensor'=4] {'tensor'}, dimensions={1}, use_global_device_ids=true | all-gather | bytes 491520 | tf_op jit(solution)/shard_map/all_gather | solution.py:166
  24.3 106.6 %while.17 = (s32[]{:T(128)}, f32[2,3,128]{2,1,0:T(4,128)S(1)}, f32[2,3,128]{2,1,0:T(4,128)S(1)}, f32[2,3,128,64]{2,3,1,0:T(8,128)S(1)}, s32[]{:T(128)}, /*index=...) while((s32[]{:T(128)}, f32[2,3,128]{2,1,0:T(4,128)S(1)}, ...), condition=%wide.region_6.7_spmd, body=%wide.region_3.6_spmd.sunk | while | flops 103517712 | bytes 7099675 | solution.py:92
  28.2 2.2 gather_fusion.1
  34.8 2.2 gather_fusion.1
  41.5 2.2 gather_fusion.1
  48.2 2.2 gather_fusion.1
  54.8 2.2 gather_fusion.1
  61.5 2.2 gather_fusion.1
  68.2 2.2 gather_fusion.1
  74.8 2.2 gather_fusion.1
  81.5 2.2 gather_fusion.1
  88.1 2.2 gather_fusion.1
  94.8 2.2 gather_fusion.1
  101.5 2.2 gather_fusion.1
  108.1 2.2 gather_fusion.1
  114.8 2.2 gather_fusion.1
  121.4 2.2 gather_fusion.1
  128.1 2.2 gather_fusion.1
  132.6 18.0 %reduce-window.6 = s32[64,8,128]{2,1,0:T(8,128)S(1)} reduce-window(s32[64,8,128]{2,1,0:T(8,128)S(1)} %fusion.33, s32[]{:T(128)} %constant.103.clone.1), window={size=1x1x128 pad=0_0x0_0x127_0}, to_apply=%region_8.9 | reduce-window | flops 8323072 | bytes 524292 | tf_op jit(solution)/shard_map/reduce-window
  151.6 30.7 %all-reduce.2.cloned.1.call-done = bf16[128,1536]{1,0:T(8,128)(2,1)} async-done(((bf16[128,1536]{1,0:T(8,128)(2,1)}), bf16[128,1536]{1,0:T(8,128)(2,1)}) %all-reduce.2.cloned.1.call-update) | async-done | bytes 393232 | tf_op jit(solution)/shard_map/psum | solution.py:199
  183.7 19.7 %scatter_custom_fusion = bf16[2048,1536]{1,0:T(8,128)(2,1)} fusion(s32[1024]{0:T(1024)S(1)} %bitcast.160, bf16[128,1536]{1,0:T(8,128)(2,1)S(1)} %fusion.18, s32[1024]{0:T(1024)S(1)} %broadcast_clamp_fusion.1, bf16[]{:T(256)} %constant.115.clone.1), kind=kCustom, calls=%fused_computation.21 | custom fusion | bytes 6291458 | tf_op jit(solution)/shard_map/scatter | solution.py:112
  203.4 151.8 %all_to_all.10 = bf16[64,32,1536]{2,1,0:T(8,128)(2,1)S(1)} all-to-all(bf16[64,32,1536]{2,1,0:T(8,128)(2,1)} %bitcast.146), channel_id=1, replica_groups=mesh['seq'=64,'tensor'=4] {'seq'}, dimensions={0} | all-to-all | bytes 12582912 | tf_op jit(solution)/shard_map/all_to_all | solution.py:203
  355.2 2.7 copy-done.2
  359.8 11.8 %convert_bitcast_fusion = bf16[64,1,32,1536]{3,2,0,1:T(8,128)(2,1)} fusion(bf16[64,32,1536]{2,1,0:T(8,128)(2,1)} %copy-done.2, f32[64,1,32,128]{3,2,0,1:T(8,128)S(1)} %convolution_bitcast_fusion.1, bf16[1,128,1536]{2,1,0:T(8,128)(2,1)S(1)} %copy-done.6, bf16[1,1536,128]{2,1,0:T(8,128)(2,1)S(1)} %copy-done.7), kind=kOutput, calls=%fused_computation.20 | convolution fusion | flops 1615331328 | bytes 14417920 | tf_op jit(solution)/shard_map/secf,efd->secd/dot_general | solution.py:119
  371.5 33.7 %copy.55 = bf16[64,1,32,1536]{2,0,1,3:T(8,128)(2,1)} copy(bf16[64,1,32,1536]{3,2,0,1:T(8,128)(2,1)} %convert_bitcast_fusion) | data formatting | bytes 12582912
  405.2 33.1 %reshape.310 = bf16[1536,2048]{1,0:T(8,128)(2,1)} reshape(bf16[1536,1,64,32]{3,2,1,0:T(8,128)(2,1)} %bitcast.144) | data formatting | bytes 12582912
  438.3 62.1 %reduce-scatter.4.cloned.1.call-done = bf16[384,2048]{1,0:T(8,128)(2,1)} async-done(((bf16[1536,2048]{1,0:T(8,128)(2,1)}), bf16[384,2048]{1,0:T(8,128)(2,1)}) %reduce-scatter.4.cloned.1.call-update) | async-done | bytes 1572880
  500.4 8.4 %reshape.311 = bf16[384,1,64,32]{3,2,1,0:T(8,128)(2,1)} reshape(bf16[384,2048]{1,0:T(8,128)(2,1)} %reduce-scatter.4.cloned.1.call-done) | data formatting | bytes 3145728
  508.8 8.7 %copy.56 = bf16[64,1,32,384]{3,2,0,1:T(8,128)(2,1)} copy(bf16[64,1,32,384]{2,0,1,3:T(8,128)(2,1)} %bitcast.147) | data formatting | bytes 3145728
  517.5 10.7 %all-to-all-start.1 = ((bf16[64,32,384]{2,1,0:T(8,128)(2,1)}), bf16[64,32,384]{2,1,0:T(8,128)(2,1)S(1)}, u32[]{:S(2)}, u32[]{:S(2)}) async-start(bf16[64,32,384]{2,1,0:T(8,128)(2,1)} %bitcast.148), calls=%async_computation.1 | async-start | bytes 3145728 | tf_op jit(solution)/shard_map/all_to_all | solution.py:126
  528.9 39.3 %all-to-all-done.1 = bf16[64,32,384]{2,1,0:T(8,128)(2,1)S(1)} async-done(((bf16[64,32,384]{2,1,0:T(8,128)(2,1)}), bf16[64,32,384]{2,1,0:T(8,128)(2,1)S(1)}, u32[]{:S(2)}, u32[]{:S(2)}) %all-to-all-start.1) | async-done | bytes 1572896 | tf_op jit(solution)/shard_map/all_to_all | solution.py:126
  568.2 3.9 gather_fusion.2
  (301 shorter events, 83.3 us)
Async XLA Ops:
  6.5 124.4 %copy-start = (bf16[384,1536]{1,0:T(8,128)(2,1)S(1)}, bf16[384,1536]{1,0:T(8,128)(2,1)}, u32[]{:S(2)}) copy-start(bf16[384,1536]{1,0:T(8,128)(2,1)} %param.23) | copy-start | bytes 3538948
  6.5 16.2 %copy-start.9 = (f32[1536]{0:T(1024)S(1)}, f32[1536]{0:T(1024)}, u32[]{:S(2)}) copy-start(f32[1536]{0:T(1024)} %param.19) | copy-start | bytes 18436
  6.5 16.2 %copy-start.12 = (bf16[1536,128]{1,0:T(8,128)(2,1)S(1)}, bf16[1536,128]{1,0:T(8,128)(2,1)}, u32[]{:S(2)}) copy-start(bf16[1536,128]{1,0:T(8,128)(2,1)} %param.21) | copy-start | bytes 1179652
  6.5 16.8 %copy-start.13 = (bf16[1536,128]{1,0:T(8,128)(2,1)S(1)}, bf16[1536,128]{1,0:T(8,128)(2,1)}, u32[]{:S(2)}) copy-start(bf16[1536,128]{1,0:T(8,128)(2,1)} %param.22) | copy-start | bytes 1179652
  6.5 175.7 %all-reduce.2.cloned.1.call-start = ((), (), s32[]{:S(2)}) async-start(), calls=%async_computation.3 | async-start | bytes 786432 | tf_op jit(solution)/shard_map/psum | solution.py:199
  20.0 3.7 copy-start.3
  22.8 1.5 copy-start.15
  130.9 1.5 copy-start.8
  131.0 51.3 %copy-start.4 = (bf16[128,1536]{1,0:T(8,128)(2,1)S(1)}, bf16[128,1536]{1,0:T(8,128)(2,1)}, u32[]{:S(2)}) copy-start(bf16[128,1536]{1,0:T(8,128)(2,1)} %copy-done.3) | copy-start | bytes 1179652
  132.1 51.4 %copy-start.10 = (f32[1536]{0:T(1024)S(1)}, f32[1536]{0:T(1024)}, u32[]{:S(2)}) copy-start(f32[1536]{0:T(1024)} %param.24) | copy-start | bytes 18436
  132.2 368.2 %reduce-scatter.4.cloned.1.call-start = ((), (), s32[]{:S(2)}) async-start(), calls=%async_computation.4 | async-start | bytes 7864320
  183.5 19.9 %copy-start.5 = (bf16[128,1536]{1,0:T(8,128)(2,1)}, bf16[128,1536]{1,0:T(8,128)(2,1)S(1)}, u32[]{:S(2)}) copy-start(bf16[128,1536]{1,0:T(8,128)(2,1)S(1)} %get-tuple-element.183) | copy-start | bytes 1179652
  203.4 154.5 %copy-start.14 = (bf16[1,1536,128]{2,1,0:T(8,128)(2,1)S(1)}, bf16[1,1536,128]{2,1,0:T(8,128)(2,1)}, u32[]{:S(2)}) copy-start(bf16[1,1536,128]{2,1,0:T(8,128)(2,1)} %param.25) | copy-start | bytes 1179652
  355.2 2.7 copy-start.2
  357.9 1.8 copy-start.6
  357.9 1.8 copy-start.7
  517.5 10.7 %copy-start.11 = (f32[128,8]{0,1:T(8,128)S(1)}, f32[128,8]{0,1:T(8,128)}, u32[]{:S(2)}) copy-start(f32[128,8]{0,1:T(8,128)} %param.33) | copy-start | bytes 12292
  517.5 50.7 %all-to-all-start.1 = ((bf16[64,32,384]{2,1,0:T(8,128)(2,1)}), bf16[64,32,384]{2,1,0:T(8,128)(2,1)S(1)}, u32[]{:S(2)}, u32[]{:S(2)}) async-start(bf16[64,32,384]{2,1,0:T(8,128)(2,1)} %bitcast.148), calls=%async_computation.1 | async-start | bytes 3145728 | tf_op jit(solution)/shard_map/all_to_all | solution.py:126
  568.2 6.9 %copy-start.1 = (bf16[384,1536]{1,0:T(8,128)(2,1)S(1)}, bf16[384,1536]{1,0:T(8,128)(2,1)}, u32[]{:S(2)}) copy-start(bf16[384,1536]{1,0:T(8,128)(2,1)} %param.23) | copy-start | bytes 3538948
Sparse Core Ops, SparseCore 0:
  132.3 49.9 all-reduce.1
  438.4 61.8 reduce-scatter.3
where the time goes:
time: 585 us; the launch traced here: 582 us
  local copies, waits for them, and re-layouts  187 us (32%)
  blocking collectives  165 us (28%)
  waiting for transfers between devices  132 us (23%)
  other arithmetic  38.9 us (7%)
  matrix products  31.2 us (5%)
  between operations  14.4 us (2%)
  starting transfers between devices  10.9 us (2%)
    all_to_all x1, blocking collectives, shards(): lax.all_to_all(pack_rows(moe_in, slot_place, CAP, expert_total), 'seq', s...  152 us
    unnamed x38, local copies, waits for them, and re-layouts  87.4 us
    gather x64, local copies, waits for them, and re-layouts, load_block(): return pool[page_index].reshape(block_span, kv_count, head_dim)  73.8 us
    unnamed x3, waiting for transfers between devices  62.1 us
    all_to_all x1, waiting for transfers between devices, finish_partial(): lax.all_to_all(expert_cols.reshape(-1, expert_cols.shape[2], col_count),...  39.3 us
    psum x1, waiting for transfers between devices, shards(): lax.psum(partial_value.astype(jnp.bfloat16), 'tensor').astype(jnp.float32)  30.7 us
    scatter x1, local copies, waits for them, and re-layouts, pack_rows(): outgoing = outgoing.at[slot_place].set(moe_in[token_rows])  19.7 us
    another operation x5, other arithmetic  18.2 us
  transfers between devices with their start and end apart: 3, of which 3 were waited for; matrix products, arithmetic and copies ran while one was open for 3% of the time, Pallas kernels for 0%

commit v1 on v0

v1 whole, which is shorter than its diff:
```python
import jax
import jax.numpy as jnp
from jax import lax
from jax.experimental import pallas as pl
from jax.experimental.pallas import tpu as pltpu
from jax.sharding import PartitionSpec as P

MESH = pl.DeviceIdType.MESH
BF16 = jnp.bfloat16
F32 = jnp.float32
HEAD = 64
NORM_EPSILON = 1e-06
MASKED_SCORE = -1e30
NX, NY, NZ = 4, 4, 8
ROWS = 128
QUARTER = ROWS // NX
HALF = QUARTER // 2
WIDTH = 1536
COLS = WIDTH // NX
AUG = WIDTH + 128
HEADS = 6
STACK = HEADS * ROWS
CACHE = 8192
BLOCK = 1024
BLOCKS = CACHE // BLOCK
PAGE = 128
FFE = 512


def whereabouts():
    seq = lax.axis_index("seq")
    x = lax.axis_index("tensor")
    core = lax.rem(seq, 2)
    y = lax.rem(lax.div(seq, 2), NY)
    z = lax.div(seq, 2 * NY)
    return x, y, z, core


def device(x, y, z, core):
    return ((z * NY + y) * 2 + core, x)


def send_to(src, dst, send_sem, recv_sem, target):
    return pltpu.make_async_remote_copy(
        src_ref=src,
        dst_ref=dst,
        send_sem=send_sem,
        recv_sem=recv_sem,
        device_id=target,
        device_id_type=MESH,
    )


def greet(targets):
    barrier = pltpu.get_barrier_semaphore()
    for target in targets:
        pl.semaphore_signal(barrier, inc=1, device_id=target, device_id_type=MESH)
    pl.semaphore_wait(barrier, len(targets))


def norm_rows(widened, gain_row):
    return (
        widened
        * lax.rsqrt(jnp.mean(widened * widened, axis=1, keepdims=True) + NORM_EPSILON)
        * gain_row
    )


def swap_halves(block):
    lane = lax.broadcasted_iota(jnp.int32, block.shape, 1)
    return jnp.where(
        lax.rem(lane, HEAD) < HEAD // 2,
        pltpu.roll(block, 128 - HEAD // 2, 1),
        pltpu.roll(block, HEAD // 2, 1),
    )


def attend_kernel(
    seen_ref,
    tokens_ref,
    cos_ref,
    sin_ref,
    routes_ref,
    gates_ref,
    attn_gain_ref,
    moe_gain_ref,
    q_hbm,
    k_hbm,
    v_hbm,
    o_hbm,
    key_pool,
    value_pool,
    gate_hbm,
    up_hbm,
    down_hbm,
    aug_ref,
    resid_ref,
    gate_all,
    up_all,
    down_all,
    tok,
    qw,
    kw,
    vw,
    ow,
    keys,
    values,
    stacked,
    best,
    total,
    mix,
    stage,
    arrived,
    partial,
    load_sem,
    key_sem,
    value_sem,
    tok_send,
    tok_recv,
    sum_send,
    sum_recv,
    w_send,
    w_recv,
):
    x, y, z, core = whereabouts()
    peers = [lax.rem(x + j, NX) for j in range(NX)]
    loads = []
    for number, (src, dst) in enumerate(
        ((q_hbm, qw), (k_hbm, kw), (v_hbm, vw), (o_hbm, ow))
    ):
        copy = pltpu.make_async_copy(src, dst, load_sem.at[number])
        copy.start()
        loads.append(copy)

    def key_copy(i):
        rows = pl.ds(pl.multiple_of(i * BLOCK, BLOCK), BLOCK)
        return pltpu.make_async_copy(
            key_pool.at[rows, :], keys.at[rows, pl.ds(0, 128)], key_sem.at[i]
        )

    def value_copy(i):
        rows = pl.ds(pl.multiple_of(i * BLOCK, BLOCK), BLOCK)
        return pltpu.make_async_copy(
            value_pool.at[rows, :], values.at[rows, :], value_sem.at[i]
        )

    for i in range(BLOCKS):
        key_copy(i).start()
        value_copy(i).start()

    greet([device(peers[j], y, z, core) for j in range(1, NX)])
    sends = []
    for j in range(1, NX):
        copy = send_to(
            tokens_ref,
            tok.at[x],
            tok_send.at[j],
            tok_recv.at[j],
            device(peers[j], y, z, core),
        )
        copy.start()
        sends.append(copy)
    tok[x] = tokens_ref[...]
    weight_waits = []
    for number, (src, dst) in enumerate(
        ((gate_hbm, gate_all), (up_hbm, up_all), (down_hbm, down_all))
    ):
        for way, j in enumerate((1, NX - 1)):
            copy = send_to(
                src,
                dst.at[x],
                w_send.at[2 * number + way],
                w_recv.at[2 * number + way],
                device(peers[j], y, z, core),
            )
            copy.start()
            sends.append(copy)
            weight_waits.append(
                send_to(
                    src,
                    dst.at[peers[NX - j]],
                    w_send.at[2 * number + way],
                    w_recv.at[2 * number + way],
                    device(peers[j], y, z, core),
                )
            )

    row = lax.broadcasted_iota(jnp.int32, (PAGE, 128), 0)
    lane = lax.broadcasted_iota(jnp.int32, (PAGE, 128), 1)

    def write_bias(p, carry):
        hidden_row = (lane == 0) & (row >= seen_ref[p])
        keys[pl.ds(pl.multiple_of(p * PAGE, PAGE), PAGE), pl.ds(128, 128)] = jnp.where(
            hidden_row, MASKED_SCORE, 0.0
        ).astype(BF16)
        return carry

    lax.fori_loop(0, CACHE // PAGE, write_bias, 0)

    for j in range(1, NX):
        send_to(
            tokens_ref,
            tok.at[peers[NX - j]],
            tok_send.at[j],
            tok_recv.at[j],
            device(peers[j], y, z, core),
        ).wait_recv()
    whole = jnp.concatenate([tok[j].astype(F32) for j in range(NX)], axis=1)
    normed = norm_rows(whole, attn_gain_ref[...]).astype(BF16)
    for copy in loads:
        copy.wait()
    cosine = cos_ref[...]
    sine = sin_ref[...]
    scale = HEAD ** (-0.5)
    queries = jnp.dot(normed, qw[...], preferred_element_type=F32)
    first_bias = jnp.where(lane == 0, 1.0, 0.0).astype(BF16)
    for pair in range(HEADS // 2):
        block = queries[:, pair * 128 : (pair + 1) * 128]
        turned = (block * cosine + swap_halves(block) * sine).astype(BF16)
        turned = turned.astype(F32) * scale
        crossed = pltpu.roll(turned, HEAD, 1)
        for side in range(2):
            head = 2 * pair + side
            group = head // 3
            placed = turned if side == group else crossed
            mine = (lane < HEAD) if group == 0 else (lane >= HEAD)
            stacked[pl.ds(head * ROWS, ROWS), pl.ds(0, 128)] = jnp.where(
                mine, placed, 0.0
            ).astype(BF16)
            stacked[pl.ds(head * ROWS, ROWS), pl.ds(128, 128)] = first_bias
    new_keys = jnp.dot(normed, kw[...], preferred_element_type=F32)
    new_keys = (new_keys * cosine + swap_halves(new_keys) * sine).astype(BF16)
    new_values = jnp.dot(normed, vw[...], preferred_element_type=F32).astype(BF16)

    scores = lax.dot_general(
        stacked[:, 0:128],
        new_keys,
        (((1,), (1,)), ((), ())),
        preferred_element_type=F32,
    )
    query_row = lax.rem(lax.broadcasted_iota(jnp.int32, (STACK, ROWS), 0), ROWS)
    key_row = lax.broadcasted_iota(jnp.int32, (STACK, ROWS), 1)
    scores = jnp.where(key_row <= query_row, scores, MASKED_SCORE)
    top = jnp.max(scores, axis=1, keepdims=True)
    weights = jnp.exp(scores - top)
    best[...] = top
    total[...] = jnp.sum(weights, axis=1, keepdims=True)
    mix[...] = jnp.dot(weights.astype(BF16), new_values, preferred_element_type=F32)

    def step(i, carry):
        key_copy(i).wait()
        value_copy(i).wait()
        rows = pl.ds(pl.multiple_of(i * BLOCK, BLOCK), BLOCK)
        scores = lax.dot_general(
            stacked[...],
            keys[rows, :],
            (((1,), (1,)), ((), ())),
            preferred_element_type=F32,
        )
        old = best[...]
        new = jnp.maximum(old, jnp.max(scores, axis=1, keepdims=True))
        shrink = jnp.exp(old - new)
        weights = jnp.exp(scores - new)
        best[...] = new
        total[...] = total[...] * shrink + jnp.sum(weights, axis=1, keepdims=True)
        mix[...] = mix[...] * shrink + jnp.dot(
            weights.astype(BF16), values[rows, :], preferred_element_type=F32
        )
        return carry

    lax.fori_loop(0, BLOCKS, step, 0)
    result = mix[...] / total[...]
    pieces = []
    for pair in range(HEADS // 2):
        sides = []
        for side in range(2):
            head = 2 * pair + side
            block = result[head * ROWS : (head + 1) * ROWS, :]
            sides.append(block if side == head // 3 else pltpu.roll(block, HEAD, 1))
        pieces.append(jnp.where(lane < HEAD, sides[0], sides[1]).astype(BF16))
    attended = jnp.concatenate(pieces, axis=1)
    summand = jnp.dot(attended, ow[...], preferred_element_type=F32)
    for j in range(NX):
        quarter = summand[j * QUARTER : (j + 1) * QUARTER, :]
        partial[j] = quarter
        stage[j] = quarter.astype(BF16)
    for j in range(1, NX):
        copy = send_to(
            stage.at[peers[j]],
            arrived.at[x],
            sum_send.at[j],
            sum_recv.at[j],
            device(peers[j], y, z, core),
        )
        copy.start()
        sends.append(copy)

    my_rows = pl.ds(pl.multiple_of(x * QUARTER, QUARTER), QUARTER)
    expert = lax.rem(lax.broadcasted_iota(jnp.int32, (QUARTER, 128), 1), 64)
    low = lax.broadcasted_iota(jnp.int32, (QUARTER, 128), 1) >= 64
    routes = routes_ref[my_rows, :]
    gates = gates_ref[my_rows, :]
    chosen = jnp.zeros((QUARTER, 128), F32)
    for k in range(routes.shape[1]):
        chosen = chosen + jnp.where(routes[:, k : k + 1] == expert, gates[:, k : k + 1], 0.0)
    high_part = chosen.astype(BF16).astype(F32)
    aug_ref[:, WIDTH:AUG] = jnp.where(low, chosen - high_part, high_part).astype(BF16)
    residual = partial[x] + jnp.concatenate(
        [tok[j, my_rows, :].astype(F32) for j in range(NX)], axis=1
    )
    for j in range(1, NX):
        send_to(
            stage.at[peers[j]],
            arrived.at[peers[NX - j]],
            sum_send.at[j],
            sum_recv.at[j],
            device(peers[j], y, z, core),
        ).wait_recv()
        residual = residual + arrived[peers[NX - j]].astype(F32)
    residual = residual.astype(BF16)
    resid_ref[...] = residual
    aug_ref[:, 0:WIDTH] = norm_rows(residual.astype(F32), moe_gain_ref[...]).astype(BF16)
    for copy in weight_waits:
        copy.wait_recv()
    for copy in sends:
        copy.wait_send()


class Gather:
    def __init__(self, size, me, target, place, halves, send_sem, recv_sem):
        self.size, self.me, self.target = size, me, target
        self.place, self.halves = place, halves
        self.send_sem, self.recv_sem = send_sem, recv_sem
        self.sent = []

    def copies(self, k, arriving):
        last = k + 1 == self.size // 2
        made = []
        for way in range(2):
            if arriving:
                shift = -(1 + k) if way == 0 else 1 + k
            else:
                shift = -k if way == 0 else k
            ref = self.place(lax.rem(self.me + shift + self.size, self.size))
            if last:
                ref = self.halves(ref)[way]
            made.append(
                send_to(
                    ref,
                    ref,
                    self.send_sem.at[way, k],
                    self.recv_sem.at[way, k],
                    self.target(1 if way == 0 else -1),
                )
            )
        return made

    def send(self, k):
        for copy in self.copies(k, False):
            copy.start()
            self.sent.append(copy)

    def wait(self, k):
        for copy in self.copies(k, True):
            copy.wait_recv()


class Scatter:
    def __init__(self, size, me, target, own, halves, stage, arrived, send_sem, recv_sem):
        self.size, self.me, self.target = size, me, target
        self.own, self.halves = own, halves
        self.stage, self.arrived = stage, arrived
        self.send_sem, self.recv_sem = send_sem, recv_sem
        self.sent = []

    def copy(self, way, k):
        src, dst = self.stage.at[way, k], self.arrived.at[way, k]
        if k == 0:
            src, dst = self.halves(src)[way], self.halves(dst)[way]
        return send_to(
            src,
            dst,
            self.send_sem.at[way, k],
            self.recv_sem.at[way, k],
            self.target(1 if way == 0 else -1),
        )

    def send(self, k):
        distance = self.size // 2 - k
        for way in range(2):
            shift = distance if way == 0 else -distance
            own = self.own(lax.rem(self.me + shift + self.size, self.size))
            here = self.stage.at[way, k]
            if k == 0:
                self.halves(here)[way][...] = self.halves(own)[way][...].astype(BF16)
            elif k == 1:
                self.copy(way, 0).wait_recv()
                came = self.halves(self.arrived.at[way, 0])[way]
                self.halves(here)[way][...] = (
                    self.halves(own)[way][...] + came[...].astype(F32)
                ).astype(BF16)
                self.halves(here)[1 - way][...] = self.halves(own)[1 - way][...].astype(BF16)
            else:
                self.copy(way, k - 1).wait_recv()
                here[...] = (own[...] + self.arrived[way, k - 1].astype(F32)).astype(BF16)
            copy = self.copy(way, k)
            copy.start()
            self.sent.append(copy)

    def result(self):
        k = self.size // 2 - 1
        answer = self.own(self.me)[...]
        for way in range(2):
            self.copy(way, k).wait_recv()
            answer = answer + self.arrived[way, k].astype(F32)
        return answer


def half_columns(ref):
    width = ref.shape[-1]
    split = (width // 256 + (width // 128) % 2) * 128
    lead = (slice(None),) * (len(ref.shape) - 1)
    return (
        ref.at[(*lead, pl.ds(0, split))],
        ref.at[(*lead, pl.ds(split, width - split))],
    )


def half_rows(ref):
    size = ref.shape[0] // 2
    return ref.at[pl.ds(0, size)], ref.at[pl.ds(size, size)]


def expert_kernel(
    aug_hbm,
    resid_ref,
    gate_hbm,
    up_hbm,
    down_hbm,
    gate_all,
    up_all,
    down_all,
    out_ref,
    rows_a,
    rows_b,
    wg,
    wu,
    wd,
    out_a,
    out_b,
    sum_a,
    sum_b,
    stage_az,
    came_az,
    stage_ay,
    came_ay,
    stage_by,
    came_by,
    stage_bz,
    came_bz,
    mixed,
    came_x,
    in_sem,
    near_sem,
    far_send,
    far_recv,
    part_send,
    part_recv,
    ay_send,
    ay_recv,
    az_send,
    az_recv,
    by_send,
    by_recv,
    bz_send,
    bz_recv,
    ry_send,
    ry_recv,
    raz_send,
    raz_recv,
    rby_send,
    rby_recv,
    rbz_send,
    rbz_recv,
    x_send,
    x_recv,
):
    x, y, z, core = whereabouts()
    x_peers = [lax.rem(x + j, NX) for j in range(NX)]
    y_peers = [lax.rem(y + j, NY) for j in range(NY)]
    z_at = lambda step: lax.rem(z + step + NZ, NZ)
    partner = device(x, y, z, 1 - core)
    greet(
        [device(x_peers[j], y, z, core) for j in range(1, NX)]
        + [device(x, y_peers[j], z, core) for j in range(1, NY)]
        + [device(x, y, z_at(1), core), device(x, y, z_at(-1), core), partner]
    )
    into_a = pltpu.make_async_copy(aug_hbm.at[pl.ds(0, HALF)], rows_a.at[z, y], in_sem.at[0])
    into_b = pltpu.make_async_copy(aug_hbm.at[pl.ds(HALF, HALF)], rows_b.at[y, z], in_sem.at[1])
    into_a.start()
    into_b.start()
    sent = []

    def columns(w, q):
        return w.at[core, :, pl.ds(pl.multiple_of(q * 128, 128), 128)]

    def depth(w, q):
        return w.at[core, pl.ds(pl.multiple_of(q * 128, 128), 128), :]

    into_a.wait()
    into_b.wait()

    for j in range(1, NY):
        copy = send_to(
            rows_a.at[z, y],
            rows_a.at[z, y],
            ay_send.at[j],
            ay_recv.at[j],
            device(x, y_peers[j], z, core),
        )
        copy.start()
        sent.append(copy)
    to_z = lambda step: device(x, y, z_at(step), core)
    to_y = lambda step: device(x, y_peers[step % NY], z, core)
    gather_az = Gather(NZ, z, to_z, lambda i: rows_a.at[i], half_rows, az_send, az_recv)
    gather_bz = Gather(NZ, z, to_z, lambda i: rows_b.at[y, i], half_columns, bz_send, bz_recv)
    gather_by = Gather(NY, y, to_y, lambda i: rows_b.at[i], half_rows, by_send, by_recv)
    gather_bz.send(0)

    far = lax.rem(x + 2, NX)
    for number, (src, dst) in enumerate(((gate_all, wg), (up_all, wu), (down_all, wd))):
        size = src.shape[1] // 2
        for way, j in enumerate((1, NX - 1)):
            q = x_peers[NX - j]
            rows = pl.ds(way * size, size)
            if number < 2:
                place = dst.at[core, rows, pl.ds(pl.multiple_of(q * 128, 128), 128)]
            else:
                place = dst.at[core, pl.ds(pl.multiple_of(q * 128 + way * size, size), size), :]
            copy = send_to(
                src.at[q, rows, :],
                place,
                far_send.at[number, way],
                far_recv.at[number, way],
                device(x_peers[j], y, z, core),
            )
            copy.start()
            sent.append(copy)
    near = []
    for number, (mine, others, dst, cut) in enumerate(
        (
            (gate_hbm, gate_all, wg, columns),
            (up_hbm, up_all, wu, columns),
            (down_hbm, down_all, wd, depth),
        )
    ):
        for which, j in enumerate((0, 1, NX - 1)):
            q = x_peers[j]
            src = mine if j == 0 else others.at[q]
            copy = pltpu.make_async_copy(src, cut(dst, q), near_sem.at[number, which])
            copy.start()
            near.append(copy)
            copy = send_to(
                src,
                cut(dst, q),
                part_send.at[number, which],
                part_recv.at[number, which],
                partner,
            )
            copy.start()
            sent.append(copy)

    for j in range(1, NY):
        place = rows_a.at[z, y_peers[NY - j]]
        send_to(
            place, place, ay_send.at[j], ay_recv.at[j], device(x, y_peers[j], z, core)
        ).wait_recv()
    gather_az.send(0)
    gather_bz.wait(0)
    gather_bz.send(1)
    gather_bz.wait(1)
    gather_bz.send(2)
    gather_az.wait(0)
    gather_az.send(1)
    gather_bz.wait(2)
    gather_bz.send(3)
    gather_bz.wait(3)
    gather_by.send(0)
    gather_az.wait(1)
    gather_az.send(2)
    gather_az.wait(2)
    gather_az.send(3)
    for number, (dst, cut) in enumerate(((wg, columns), (wu, columns), (wd, depth))):
        size = (WIDTH if number < 2 else 128) // 2
        for way, j in enumerate((1, NX - 1)):
            rows = pl.ds(way * size, size)
            if number < 2:
                place = dst.at[core, rows, pl.ds(pl.multiple_of(far * 128, 128), 128)]
            else:
                place = dst.at[core, pl.ds(pl.multiple_of(far * 128 + way * size, size), size), :]
            send_to(
                place,
                place,
                far_send.at[number, way],
                far_recv.at[number, way],
                device(x_peers[j], y, z, core),
            ).wait_recv()
        copy = send_to(
            cut(dst, far),
            cut(dst, far),
            part_send.at[number, 3],
            part_recv.at[number, 3],
            partner,
        )
        copy.start()
        sent.append(copy)
    gather_by.wait(0)
    gather_by.send(1)
    gather_az.wait(3)
    for copy in near:
        copy.wait()

    def partner_columns(w, q):
        return w.at[1 - core, :, pl.ds(pl.multiple_of(q * 128, 128), 128)]

    def partner_depth(w, q):
        return w.at[1 - core, pl.ds(pl.multiple_of(q * 128, 128), 128), :]

    for number, (dst, cut) in enumerate(
        ((wg, partner_columns), (wu, partner_columns), (wd, partner_depth))
    ):
        for which, j in enumerate((0, 1, NX - 1, 2)):
            place = cut(dst, x_peers[j])
            send_to(
                place,
                place,
                part_send.at[number, which],
                part_recv.at[number, which],
                partner,
            ).wait_recv()

    first_expert = 2 * (z * NY + y)

    def compute(rows, out, steps):
        lead = rows.shape[0] // steps
        count = lead * rows.shape[1] * rows.shape[2]

        def chunk(i, carry):
            part = pl.ds(i * lead, lead)
            block = rows[part].reshape(count, AUG)
            inputs = block[:, 0:WIDTH]
            gates = block[:, WIDTH:AUG].astype(F32)
            lane = lax.rem(lax.broadcasted_iota(jnp.int32, (count, 128), 1), 64)
            answer = None
            for e in range(2):
                gate = jnp.sum(
                    jnp.where(lane == first_expert + e, gates, 0.0), axis=1, keepdims=True
                )
                gate_act = jnp.dot(inputs, wg[e], preferred_element_type=F32)
                up_act = jnp.dot(inputs, wu[e], preferred_element_type=F32)
                hidden = (gate_act / (1.0 + jnp.exp(-gate_act)) * up_act * gate).astype(BF16)
                term = jnp.dot(hidden, wd[e], preferred_element_type=F32)
                answer = term if answer is None else answer + term
            out[part] = answer.reshape(lead, rows.shape[1], rows.shape[2], WIDTH)
            return carry

        lax.fori_loop(0, steps, chunk, 0)

    scatter_az = Scatter(
        NZ, z, to_z, lambda i: out_a.at[i], half_rows, stage_az, came_az, raz_send, raz_recv
    )
    scatter_by = Scatter(
        NY, y, to_y, lambda i: out_b.at[i], half_rows, stage_by, came_by, rby_send, rby_recv
    )
    scatter_bz = Scatter(
        NZ, z, to_z, lambda i: sum_b.at[i], half_columns, stage_bz, came_bz, rbz_send, rbz_recv
    )
    compute(rows_a, out_a, 2)
    scatter_az.send(0)
    gather_by.wait(1)
    compute(rows_b, out_b, 2)
    scatter_by.send(0)
    scatter_az.send(1)
    scatter_by.send(1)
    scatter_az.send(2)
    scatter_az.send(3)
    sum_b[...] = scatter_by.result()
    scatter_bz.send(0)
    sum_a[...] = scatter_az.result()
    stage_ay[...] = sum_a[...].astype(BF16)
    for j in range(1, NY):
        copy = send_to(
            stage_ay.at[y_peers[j]],
            came_ay.at[y],
            ry_send.at[j],
            ry_recv.at[j],
            device(x, y_peers[j], z, core),
        )
        copy.start()
        sent.append(copy)
    scatter_bz.send(1)
    scatter_bz.send(2)
    scatter_bz.send(3)
    upper = sum_a[y]
    for j in range(1, NY):
        send_to(
            stage_ay.at[y_peers[j]],
            came_ay.at[y_peers[NY - j]],
            ry_send.at[j],
            ry_recv.at[j],
            device(x, y_peers[j], z, core),
        ).wait_recv()
        upper = upper + came_ay[y_peers[NY - j]].astype(F32)
    lower = scatter_bz.result()
    answer = resid_ref[...].astype(F32) + jnp.concatenate([upper, lower], axis=0)
    answer = answer.astype(BF16)
    for j in range(NX):
        mixed[j] = answer[:, j * COLS : (j + 1) * COLS]
    for j in range(1, NX):
        copy = send_to(
            mixed.at[x_peers[j]],
            came_x.at[x],
            x_send.at[j],
            x_recv.at[j],
            device(x_peers[j], y, z, core),
        )
        copy.start()
        sent.append(copy)
    out_ref[pl.ds(pl.multiple_of(x * QUARTER, QUARTER), QUARTER), :] = mixed[x]
    for j in range(1, NX):
        source = x_peers[NX - j]
        send_to(
            mixed.at[x_peers[j]],
            came_x.at[source],
            x_send.at[j],
            x_recv.at[j],
            device(x_peers[j], y, z, core),
        ).wait_recv()
        out_ref[pl.ds(pl.multiple_of(source * QUARTER, QUARTER), QUARTER), :] = came_x[source]
    for copy in sent:
        copy.wait_send()
    for ring in (
        gather_az,
        gather_bz,
        gather_by,
        scatter_az,
        scatter_by,
        scatter_bz,
    ):
        for copy in ring.sent:
            copy.wait_send()


def shards(
    tokens,
    attn_gain,
    q_weight,
    key_matrix,
    value_matrix,
    o_weight,
    moe_gain,
    gate_weight,
    up_weight,
    down_weight,
    key_page_pool,
    value_page_pool,
    cache_lens,
    page_table,
    routes,
    route_gates,
):
    vmem = pl.BlockSpec(memory_space=pltpu.VMEM)
    smem = pl.BlockSpec(memory_space=pltpu.SMEM)
    hbm = pl.BlockSpec(memory_space=pl.ANY)
    dma = pltpu.SemaphoreType.DMA
    length = cache_lens[0]
    page = jnp.arange(CACHE // PAGE, dtype=jnp.int32)
    position = jnp.sum(jnp.where(page_table[0][None, :] == page[:, None], page[None, :], 0), axis=1)
    seen = length - position * PAGE
    half = HEAD // 2
    frequency = 10000.0 ** (-2.0 * jnp.arange(half, dtype=F32) / HEAD)
    places = (length + jnp.arange(ROWS, dtype=jnp.int32)).astype(F32)
    angle = places[:, None] * frequency
    cosine = jnp.tile(jnp.cos(angle), (1, 4))
    sine = jnp.sin(angle)
    sine = jnp.concatenate([-sine, sine, -sine, sine], axis=1)
    shape = jax.ShapeDtypeStruct
    gate_own, up_own, down_own = gate_weight[0], up_weight[0], down_weight[0]
    aug, resid, gate_all, up_all, down_all = pl.pallas_call(
        attend_kernel,
        out_shape=(
            shape((QUARTER, AUG), BF16),
            shape((QUARTER, WIDTH), BF16),
            shape((NX, WIDTH, 128), BF16),
            shape((NX, WIDTH, 128), BF16),
            shape((NX, 128, WIDTH), BF16),
        ),
        in_specs=[smem] + [vmem] * 7 + [hbm] * 9,
        out_specs=(vmem, vmem, hbm, hbm, hbm),
        scratch_shapes=[
            pltpu.VMEM((NX, ROWS, COLS), BF16),
            pltpu.VMEM((WIDTH, COLS), BF16),
            pltpu.VMEM((WIDTH, 128), BF16),
            pltpu.VMEM((WIDTH, 128), BF16),
            pltpu.VMEM((COLS, WIDTH), BF16),
            pltpu.VMEM((CACHE, 256), BF16),
            pltpu.VMEM((CACHE, 128), BF16),
            pltpu.VMEM((STACK, 256), BF16),
            pltpu.VMEM((STACK, 1), F32),
            pltpu.VMEM((STACK, 1), F32),
            pltpu.VMEM((STACK, 128), F32),
            pltpu.VMEM((NX, QUARTER, WIDTH), BF16),
            pltpu.VMEM((NX, QUARTER, WIDTH), BF16),
            pltpu.VMEM((NX, QUARTER, WIDTH), F32),
            dma((4,)),
            dma((BLOCKS,)),
            dma((BLOCKS,)),
            dma((NX,)),
            dma((NX,)),
            dma((NX,)),
            dma((NX,)),
            dma((6,)),
            dma((6,)),
        ],
        compiler_params=pltpu.CompilerParams(
            collective_id=0, has_side_effects=True, vmem_limit_bytes=60 << 20
        ),
        name="attend",
    )(
        seen,
        tokens,
        cosine,
        sine,
        routes,
        route_gates,
        attn_gain.reshape(1, WIDTH),
        moe_gain.reshape(1, WIDTH),
        q_weight,
        key_matrix,
        value_matrix,
        o_weight,
        key_page_pool.reshape(CACHE, 128),
        value_page_pool.reshape(CACHE, 128),
        gate_own,
        up_own,
        down_own,
    )
    pair = lambda *dims: pltpu.VMEM((2, *dims), BF16)
    return pl.pallas_call(
        expert_kernel,
        out_shape=shape((ROWS, COLS), BF16),
        in_specs=[hbm, vmem] + [hbm] * 6,
        out_specs=vmem,
        scratch_shapes=[
            pltpu.VMEM((NZ, NY, HALF, AUG), BF16),
            pltpu.VMEM((NY, NZ, HALF, AUG), BF16),
            pair(WIDTH, FFE),
            pair(WIDTH, FFE),
            pair(FFE, WIDTH),
            pltpu.VMEM((NZ, NY, HALF, WIDTH), F32),
            pltpu.VMEM((NY, NZ, HALF, WIDTH), F32),
            pltpu.VMEM((NY, HALF, WIDTH), F32),
            pltpu.VMEM((NZ, HALF, WIDTH), F32),
            pair(NZ // 2, NY, HALF, WIDTH),
            pair(NZ // 2, NY, HALF, WIDTH),
            pltpu.VMEM((NY, HALF, WIDTH), BF16),
            pltpu.VMEM((NY, HALF, WIDTH), BF16),
            pair(NY // 2, NZ, HALF, WIDTH),
            pair(NY // 2, NZ, HALF, WIDTH),
            pair(NZ // 2, HALF, WIDTH),
            pair(NZ // 2, HALF, WIDTH),
            pltpu.VMEM((NX, QUARTER, COLS), BF16),
            pltpu.VMEM((NX, QUARTER, COLS), BF16),
            dma((2,)),
            dma((3, 3)),
            dma((3, 2)),
            dma((3, 2)),
            dma((3, 4)),
            dma((3, 4)),
            dma((NY,)),
            dma((NY,)),
            dma((2, NZ // 2)),
            dma((2, NZ // 2)),
            dma((2, NY // 2)),
            dma((2, NY // 2)),
            dma((2, NZ // 2)),
            dma((2, NZ // 2)),
            dma((NY,)),
            dma((NY,)),
            dma((2, NZ // 2)),
            dma((2, NZ // 2)),
            dma((2, NY // 2)),
            dma((2, NY // 2)),
            dma((2, NZ // 2)),
            dma((2, NZ // 2)),
            dma((NX,)),
            dma((NX,)),
        ],
        compiler_params=pltpu.CompilerParams(
            collective_id=1, has_side_effects=True, vmem_limit_bytes=60 << 20
        ),
        name="experts",
    )(aug, resid, gate_own, up_own, down_own, gate_all, up_all, down_all)


def solution(mesh):
    in_specs = (
        P("seq", "tensor"),
        P(),
        P(None, "tensor"),
        P(None, "tensor"),
        P(None, "tensor"),
        P("tensor", None),
        P(),
        P("seq", None, "tensor"),
        P("seq", None, "tensor"),
        P("seq", "tensor", None),
        P("seq", None, "tensor"),
        P("seq", None, "tensor"),
        P("seq"),
        P("seq", None),
        P("seq", None),
        P("seq", None),
    )
    out_specs = P("seq", "tensor")
    return jax.shard_map(shards, mesh=mesh, in_specs=in_specs, out_specs=out_specs, check_vma=False)
```

time: 585 us -> 137 us (0.23)
  local copies, waits for them, and re-layouts: 187 us -> 7.76 us
  blocking collectives: 165 us -> 0 us
  waiting for transfers between devices: 132 us -> 0 us
  Pallas kernels: 0 us -> 125 us
  other arithmetic: 38.9 us -> 2.39 us
  matrix products: 31.2 us -> 0 us
  between operations: 14.4 us -> 0.69 us
  starting transfers between devices: 10.9 us -> 0 us
    all_to_all x1 -> x0, blocking collectives: 152 us -> none  [shards(): lax.all_to_all(pack_rows(moe_in, slot_place, CAP, expert_total), 'seq', s...]
    pallas_call x0 -> x2, Pallas kernels: none -> 125 us  [the longest x1 83.1 us: shards(): pl.pallas_call(expert_kernel, out_shape=shape((ROWS, COLS), BF16), in_spe...]
    unnamed x38 -> x3, local copies, waits for them, and re-layouts: 87.4 us -> 4.36 us
    gather x65 -> x0, local copies, waits for them, and re-layouts: 77.7 us -> none  [the longest x64 73.8 us: load_block(): return pool[page_index].reshape(block_span, kv_count, head_dim)]
    unnamed x3 -> x0, waiting for transfers between devices: 62.1 us -> none
    all_to_all x1 -> x0, waiting for transfers between devices: 39.3 us -> none  [finish_partial(): lax.all_to_all(expert_cols.reshape(-1, expert_cols.shape[2], col_count),...]
    dot_general x40 -> x0, matrix products: 31.2 us -> none  [the longest x1 11.8 us: finish_partial(): jnp.einsum('secf,efd->secd', hidden, down_weight, preferred_element_type=...]
    psum x1 -> x0, waiting for transfers between devices: 30.7 us -> none  [shards(): lax.psum(partial_value.astype(jnp.bfloat16), 'tensor').astype(jnp.float32)]
  transfers between devices with their start and end apart: 3 -> 0, of which waited for: 3 -> 0; matrix products, arithmetic and copies ran while one was open for 3% -> 0% of each run, Pallas kernels for 0% -> 0%
where the time goes in v1:
time: 137 us; the launch traced here: 136 us
  Pallas kernels  125 us (91%)
  local copies, waits for them, and re-layouts  7.76 us (6%)
  other arithmetic  2.39 us (2%)
    pallas_call x1, Pallas kernels, shards(): pl.pallas_call(expert_kernel, out_shape=shape((ROWS, COLS), BF16), in_spe...  83.1 us
    pallas_call x1, Pallas kernels, shards(): pl.pallas_call(attend_kernel, out_shape=(shape((QUARTER, AUG), BF16), sha...  41.6 us
    unnamed x3, local copies, waits for them, and re-layouts  4.36 us

profile of v1, /device:TPU:8, one launch (start us, length us, event | category | flops | bytes accessed | tf_op | source)
XLA Modules:
  0.0 135.6 jit_solution(2275815072485411198)
XLA Ops:
  0.7 0.8 select_reduce_fusion
  1.4 0.6 multiply_subtract_fusion.seen_ref
  2.0 1.3 reshape.52.attn_gain_ref
  3.3 1.3 reshape.53.moe_gain_ref
  4.6 1.4 %copy.30.routes_ref = s32[128,8]{1,0:T(8,128)} copy(s32[128,8]{0,1:T(8,128)} %param.30) | data formatting | bytes 8192 | tf_op args[14]
  6.0 1.4 %copy.31.gates_ref = f32[128,8]{1,0:T(8,128)} copy(f32[128,8]{0,1:T(8,128)} %param.31) | data formatting | bytes 8192 | tf_op args[15]
  7.4 0.3 fusion
  7.7 0.8 pad_maximum_fusion.sin_ref
  8.5 0.1 copy.28
  8.6 0.7 copy.29.cos_ref
  9.3 41.6 %attend.1 = (bf16[32,1664]{1,0:T(8,128)(2,1)}, bf16[32,1536]{1,0:T(8,128)(2,1)}, bf16[4,1536,128]{2,1,0:T(8,128)(2,1)}, bf16[4,1536,128]{2,1,0:T(8,128)(2,1)}, bf16[4,128,1536]{2,1,0:T(8,128)(2,1)}) custom-call(s32[64]{0:T(128)} %multiply_subtract_fusion.seen_ref, bf16[128,384]{1,0:T(8,128)(2,1)} %tokens_ref.1, f32[128,128]{1,0:T(8,128)} %copy.29.cos_ref, ...), custom_call_target="tpu_custom_call" | custom-call | tf_op jit(solution)/shard_map/attend/pallas_call | solution.py:789
  50.9 83.1 %experts.1 = bf16[128,384]{1,0:T(8,128)(2,1)} custom-call(bf16[32,1664]{1,0:T(8,128)(2,1)} %get-tuple-element.10.aug_hbm, bf16[32,1536]{1,0:T(8,128)(2,1)} %get-tuple-element.11.resid_ref, bf16[1536,128]{1,0:T(8,128)(2,1)} %bitcast.13, bf16[1536,128]{1,0:T(8,128)(2,1)} %bitcast.15, bf16[128,1536]{1,0:T(8,128)(2,1)} %bitcast.17, ...), custom_call_target="tpu_custom_call" | custom-call | tf_op jit(solution)/shard_map/experts/pallas_call | solution.py:849
  134.0 1.5 %copy.34 = bf16[128,384]{1,0:T(8,128)(2,1)} copy(bf16[128,384]{1,0:T(8,128)(2,1)} %experts.1) | data formatting | bytes 196608
  (3 shorter events, 0.0 us)

commit v2 on v1

v2 whole, which is shorter than its diff:
```python
import jax
import jax.numpy as jnp
from jax import lax
from jax.experimental import pallas as pl
from jax.experimental.pallas import tpu as pltpu
from jax.sharding import PartitionSpec as P

MESH = pl.DeviceIdType.MESH
BF16 = jnp.bfloat16
F32 = jnp.float32
HEAD = 64
NORM_EPSILON = 1e-06
MASKED_SCORE = -1e30
NX, NY, NZ = 4, 4, 8
ROWS = 128
QUARTER = ROWS // NX
HALF = QUARTER // 2
WIDTH = 1536
COLS = WIDTH // NX
AUG = WIDTH + 128
HEADS = 6
STACK = HEADS * ROWS
CACHE = 8192
BLOCK = 1024
BLOCKS = CACHE // BLOCK
PAGE = 128
FFE = 512


def whereabouts():
    seq = lax.axis_index("seq")
    x = lax.axis_index("tensor")
    core = lax.rem(seq, 2)
    y = lax.rem(lax.div(seq, 2), NY)
    z = lax.div(seq, 2 * NY)
    return x, y, z, core


def device(x, y, z, core):
    return ((z * NY + y) * 2 + core, x)


def send_to(src, dst, send_sem, recv_sem, target):
    return pltpu.make_async_remote_copy(
        src_ref=src,
        dst_ref=dst,
        send_sem=send_sem,
        recv_sem=recv_sem,
        device_id=target,
        device_id_type=MESH,
    )


def greet(targets):
    barrier = pltpu.get_barrier_semaphore()
    for target in targets:
        pl.semaphore_signal(barrier, inc=1, device_id=target, device_id_type=MESH)
    pl.semaphore_wait(barrier, len(targets))


def norm_rows(widened, gain_row):
    return (
        widened
        * lax.rsqrt(jnp.mean(widened * widened, axis=1, keepdims=True) + NORM_EPSILON)
        * gain_row
    )


def swap_halves(block):
    lane = lax.broadcasted_iota(jnp.int32, block.shape, 1)
    return jnp.where(
        lax.rem(lane, HEAD) < HEAD // 2,
        pltpu.roll(block, 128 - HEAD // 2, 1),
        pltpu.roll(block, HEAD // 2, 1),
    )


class Gather:
    def __init__(self, size, me, target, place, halves, send_sem, recv_sem):
        self.size, self.me, self.target = size, me, target
        self.place, self.halves = place, halves
        self.send_sem, self.recv_sem = send_sem, recv_sem
        self.sent = []

    def copies(self, k, arriving):
        last = k + 1 == self.size // 2
        made = []
        for way in range(2):
            if arriving:
                shift = -(1 + k) if way == 0 else 1 + k
            else:
                shift = -k if way == 0 else k
            ref = self.place(lax.rem(self.me + shift + self.size, self.size))
            if last:
                ref = self.halves(ref)[way]
            made.append(
                send_to(
                    ref,
                    ref,
                    self.send_sem.at[way, k],
                    self.recv_sem.at[way, k],
                    self.target(1 if way == 0 else -1),
                )
            )
        return made

    def send(self, k):
        for copy in self.copies(k, False):
            copy.start()
            self.sent.append(copy)

    def wait(self, k):
        for copy in self.copies(k, True):
            copy.wait_recv()


class Scatter:
    def __init__(self, size, me, target, own, halves, stage, arrived, send_sem, recv_sem):
        self.size, self.me, self.target = size, me, target
        self.own, self.halves = own, halves
        self.stage, self.arrived = stage, arrived
        self.send_sem, self.recv_sem = send_sem, recv_sem
        self.sent = []

    def copy(self, way, k):
        src, dst = self.stage.at[way, k], self.arrived.at[way, k]
        if k == 0:
            src, dst = self.halves(src)[way], self.halves(dst)[way]
        return send_to(
            src,
            dst,
            self.send_sem.at[way, k],
            self.recv_sem.at[way, k],
            self.target(1 if way == 0 else -1),
        )

    def send(self, k):
        distance = self.size // 2 - k
        for way in range(2):
            shift = distance if way == 0 else -distance
            own = self.own(lax.rem(self.me + shift + self.size, self.size))
            here = self.stage.at[way, k]
            if k == 0:
                self.halves(here)[way][...] = self.halves(own)[way][...].astype(BF16)
            elif k == 1:
                self.copy(way, 0).wait_recv()
                came = self.halves(self.arrived.at[way, 0])[way]
                self.halves(here)[way][...] = (
                    self.halves(own)[way][...] + came[...].astype(F32)
                ).astype(BF16)
                self.halves(here)[1 - way][...] = self.halves(own)[1 - way][...].astype(BF16)
            else:
                self.copy(way, k - 1).wait_recv()
                here[...] = (own[...] + self.arrived[way, k - 1].astype(F32)).astype(BF16)
            copy = self.copy(way, k)
            copy.start()
            self.sent.append(copy)

    def result(self):
        k = self.size // 2 - 1
        answer = self.own(self.me)[...]
        for way in range(2):
            self.copy(way, k).wait_recv()
            answer = answer + self.arrived[way, k].astype(F32)
        return answer


def half_columns(ref):
    width = ref.shape[-1]
    split = (width // 256 + (width // 128) % 2) * 128
    lead = (slice(None),) * (len(ref.shape) - 1)
    return (
        ref.at[(*lead, pl.ds(0, split))],
        ref.at[(*lead, pl.ds(split, width - split))],
    )


def half_rows(ref):
    size = ref.shape[0] // 2
    return ref.at[pl.ds(0, size)], ref.at[pl.ds(size, size)]


def layer_kernel(
    length_ref,
    table_ref,
    tokens_ref,
    cos_ref,
    sin_ref,
    routes_ref,
    gates_ref,
    attn_gain_ref,
    moe_gain_ref,
    q_hbm,
    k_hbm,
    v_hbm,
    o_hbm,
    key_pool,
    value_pool,
    gate_hbm,
    up_hbm,
    down_hbm,
    out_ref,
    tok,
    qw,
    kw,
    vw,
    ow,
    keys,
    values,
    stacked,
    best,
    total,
    mix,
    stage,
    arrived,
    partial,
    route_rows,
    resid,
    rows_a,
    rows_b,
    wg,
    wu,
    wd,
    out_a,
    out_b,
    sum_a,
    sum_b,
    stage_az,
    came_az,
    stage_ay,
    came_ay,
    stage_by,
    came_by,
    stage_bz,
    came_bz,
    mixed,
    came_x,
    load_sem,
    key_sem,
    value_sem,
    tok_send,
    tok_recv,
    sum_send,
    sum_recv,
    own_sem,
    near_send,
    near_recv,
    far_send,
    far_recv,
    part_send,
    part_recv,
    ay_send,
    ay_recv,
    az_send,
    az_recv,
    by_send,
    by_recv,
    bz_send,
    bz_recv,
    ry_send,
    ry_recv,
    raz_send,
    raz_recv,
    rby_send,
    rby_recv,
    rbz_send,
    rbz_recv,
    x_send,
    x_recv,
):
    x, y, z, core = whereabouts()
    peers = [lax.rem(x + j, NX) for j in range(NX)]
    y_peers = [lax.rem(y + j, NY) for j in range(NY)]
    z_at = lambda step: lax.rem(z + step + NZ, NZ)
    partner = device(x, y, z, 1 - core)
    sent = []
    loads = []
    for number, (src, dst) in enumerate(
        ((q_hbm, qw), (k_hbm, kw), (v_hbm, vw), (o_hbm, ow))
    ):
        copy = pltpu.make_async_copy(src, dst, load_sem.at[number])
        copy.start()
        loads.append(copy)

    def key_copy(i):
        rows = pl.ds(pl.multiple_of(i * BLOCK, BLOCK), BLOCK)
        return pltpu.make_async_copy(
            key_pool.at[rows, :], keys.at[rows, pl.ds(0, 128)], key_sem.at[i]
        )

    def value_copy(i):
        rows = pl.ds(pl.multiple_of(i * BLOCK, BLOCK), BLOCK)
        return pltpu.make_async_copy(
            value_pool.at[rows, :], values.at[rows, :], value_sem.at[i]
        )

    for i in range(BLOCKS):
        key_copy(i).start()
        value_copy(i).start()

    greet(
        [device(peers[j], y, z, core) for j in range(1, NX)]
        + [device(x, y_peers[j], z, core) for j in range(1, NY)]
        + [device(x, y, z_at(1), core), device(x, y, z_at(-1), core), partner]
    )
    for j in range(1, NX):
        copy = send_to(
            tokens_ref,
            tok.at[x],
            tok_send.at[j],
            tok_recv.at[j],
            device(peers[j], y, z, core),
        )
        copy.start()
        sent.append(copy)
    tok[x] = tokens_ref[...]

    weights = ((gate_hbm, wg), (up_hbm, wu), (down_hbm, wd))

    def part_of(number, owner, q, way=None):
        w = weights[number][1]
        size = (128 if number == 2 else WIDTH) // (1 if way is None else 2)
        first = 0 if way is None else way * size
        if number == 2:
            return w.at[owner, pl.ds(pl.multiple_of(q * 128 + first, 64), size), :]
        return w.at[owner, pl.ds(first, size), pl.ds(pl.multiple_of(q * 128, 128), 128)]

    def own_copy(number):
        return pltpu.make_async_copy(
            weights[number][0], part_of(number, core, x), own_sem.at[number]
        )

    def near_copy(number, way, q):
        return send_to(
            weights[number][0],
            part_of(number, core, q),
            near_send.at[number, way],
            near_recv.at[number, way],
            device(peers[(1, NX - 1)[way]], y, z, core),
        )

    def far_copy(number, way, q):
        place = part_of(number, core, q, way)
        return send_to(
            place,
            place,
            far_send.at[number, way],
            far_recv.at[number, way],
            device(peers[(1, NX - 1)[way]], y, z, core),
        )

    def part_copy(number, which, owner, src=None):
        place = part_of(number, owner, peers[which])
        return send_to(
            place if src is None else src,
            place,
            part_send.at[number, which],
            part_recv.at[number, which],
            partner,
        )

    def begin(copy):
        copy.start()
        sent.append(copy)

    def send_near(number):
        own_copy(number).start()
        for way in range(2):
            begin(near_copy(number, way, x))
        begin(part_copy(number, 0, core, weights[number][0]))

    def send_far(number):
        for way, q in ((0, peers[NX - 1]), (1, peers[1])):
            near_copy(number, way, q).wait_recv()
            begin(far_copy(number, way, q))
        begin(part_copy(number, 1, core))
        begin(part_copy(number, NX - 1, core))

    def share_far(number):
        for way in range(2):
            far_copy(number, way, peers[2]).wait_recv()
        begin(part_copy(number, 2, core))

    def settle(number):
        own_copy(number).wait()
        for which in range(NX):
            part_copy(number, which, 1 - core).wait_recv()

    send_near(0)
    send_near(1)

    row = lax.broadcasted_iota(jnp.int32, (PAGE, 128), 0)
    lane = lax.broadcasted_iota(jnp.int32, (PAGE, 128), 1)
    pages = CACHE // PAGE
    pool_page = lax.broadcasted_iota(jnp.int32, (pages, pages), 0)
    cache_page = lax.broadcasted_iota(jnp.int32, (pages, pages), 1)
    position = jnp.sum(
        jnp.where(table_ref[...] == pool_page, cache_page, 0).astype(F32),
        axis=1,
        keepdims=True,
    ).astype(jnp.int32)
    seen = length_ref[0] - position * PAGE
    for p in range(pages):
        hidden_row = (lane == 0) & (row >= seen[p : p + 1, :])
        keys[p * PAGE : (p + 1) * PAGE, 128:256] = jnp.where(
            hidden_row, MASKED_SCORE, 0.0
        ).astype(BF16)

    expert = lax.rem(row, 64)
    chosen = jnp.zeros((128, ROWS), F32)
    for k in range(routes_ref.shape[0]):
        chosen = chosen + jnp.where(
            routes_ref[k : k + 1, :] == expert, gates_ref[k : k + 1, :], 0.0
        )
    high_part = chosen.astype(BF16).astype(F32)
    route_rows[...] = jnp.where(row >= 64, chosen - high_part, high_part).T

    for j in range(1, NX):
        send_to(
            tokens_ref,
            tok.at[peers[NX - j]],
            tok_send.at[j],
            tok_recv.at[j],
            device(peers[j], y, z, core),
        ).wait_recv()
    whole = jnp.concatenate([tok[j].astype(F32) for j in range(NX)], axis=1)
    normed = norm_rows(whole, attn_gain_ref[...].reshape(1, WIDTH)).astype(BF16)
    for copy in loads:
        copy.wait()
    cosine = cos_ref[...]
    sine = sin_ref[...]
    scale = HEAD ** (-0.5)
    queries = jnp.dot(normed, qw[...], preferred_element_type=F32)
    first_bias = jnp.where(lane == 0, 1.0, 0.0).astype(BF16)
    for pair in range(HEADS // 2):
        block = queries[:, pair * 128 : (pair + 1) * 128]
        turned = (block * cosine + swap_halves(block) * sine).astype(BF16)
        turned = turned.astype(F32) * scale
        crossed = pltpu.roll(turned, HEAD, 1)
        for side in range(2):
            head = 2 * pair + side
            group = head // 3
            placed = turned if side == group else crossed
            mine = (lane < HEAD) if group == 0 else (lane >= HEAD)
            stacked[pl.ds(head * ROWS, ROWS), pl.ds(0, 128)] = jnp.where(
                mine, placed, 0.0
            ).astype(BF16)
            stacked[pl.ds(head * ROWS, ROWS), pl.ds(128, 128)] = first_bias
    new_keys = jnp.dot(normed, kw[...], preferred_element_type=F32)
    new_keys = (new_keys * cosine + swap_halves(new_keys) * sine).astype(BF16)
    new_values = jnp.dot(normed, vw[...], preferred_element_type=F32).astype(BF16)

    scores = lax.dot_general(
        stacked[:, 0:128],
        new_keys,
        (((1,), (1,)), ((), ())),
        preferred_element_type=F32,
    )
    query_row = lax.rem(lax.broadcasted_iota(jnp.int32, (STACK, ROWS), 0), ROWS)
    key_row = lax.broadcasted_iota(jnp.int32, (STACK, ROWS), 1)
    scores = jnp.where(key_row <= query_row, scores, MASKED_SCORE)
    top = jnp.max(scores, axis=1, keepdims=True)
    odds = jnp.exp(scores - top)
    best[...] = top
    total[...] = jnp.sum(odds, axis=1, keepdims=True)
    mix[...] = jnp.dot(odds.astype(BF16), new_values, preferred_element_type=F32)

    def step(i, carry):
        key_copy(i).wait()
        value_copy(i).wait()
        rows = pl.ds(pl.multiple_of(i * BLOCK, BLOCK), BLOCK)
        scores = lax.dot_general(
            stacked[...],
            keys[rows, :],
            (((1,), (1,)), ((), ())),
            preferred_element_type=F32,
        )
        old = best[...]
        new = jnp.maximum(old, jnp.max(scores, axis=1, keepdims=True))
        shrink = jnp.exp(old - new)
        odds = jnp.exp(scores - new)
        best[...] = new
        total[...] = total[...] * shrink + jnp.sum(odds, axis=1, keepdims=True)
        mix[...] = mix[...] * shrink + jnp.dot(
            odds.astype(BF16), values[rows, :], preferred_element_type=F32
        )
        return carry

    lax.fori_loop(0, 4, step, 0)
    send_far(0)
    send_near(2)
    lax.fori_loop(4, 7, step, 0)
    send_far(1)
    lax.fori_loop(7, BLOCKS, step, 0)
    result = mix[...] / total[...]
    pieces = []
    for pair in range(HEADS // 2):
        sides = []
        for side in range(2):
            head = 2 * pair + side
            block = result[head * ROWS : (head + 1) * ROWS, :]
            sides.append(block if side == head // 3 else pltpu.roll(block, HEAD, 1))
        pieces.append(jnp.where(lane < HEAD, sides[0], sides[1]).astype(BF16))
    attended = jnp.concatenate(pieces, axis=1)
    summand = jnp.dot(attended, ow[...], preferred_element_type=F32)
    for j in range(NX):
        quarter = summand[j * QUARTER : (j + 1) * QUARTER, :]
        partial[j] = quarter
        stage[j] = quarter.astype(BF16)
    for j in range(1, NX):
        copy = send_to(
            stage.at[peers[j]],
            arrived.at[x],
            sum_send.at[j],
            sum_recv.at[j],
            device(peers[j], y, z, core),
        )
        copy.start()
        sent.append(copy)

    my_rows = pl.ds(pl.multiple_of(x * QUARTER, QUARTER), QUARTER)
    residual = partial[x] + jnp.concatenate(
        [tok[j, my_rows, :].astype(F32) for j in range(NX)], axis=1
    )
    for j in range(1, NX):
        send_to(
            stage.at[peers[j]],
            arrived.at[peers[NX - j]],
            sum_send.at[j],
            sum_recv.at[j],
            device(peers[j], y, z, core),
        ).wait_recv()
        residual = residual + arrived[peers[NX - j]].astype(F32)
    residual = residual.astype(BF16)
    resid[...] = residual
    moe_in = norm_rows(residual.astype(F32), moe_gain_ref[...].reshape(1, WIDTH)).astype(BF16)
    augmented = jnp.concatenate([moe_in, route_rows[my_rows, :].astype(BF16)], axis=1)
    rows_a[z, y] = augmented[0:HALF]
    rows_b[y, z] = augmented[HALF:QUARTER]

    for j in range(1, NY):
        begin(
            send_to(
                rows_a.at[z, y],
                rows_a.at[z, y],
                ay_send.at[j],
                ay_recv.at[j],
                device(x, y_peers[j], z, core),
            )
        )
    to_z = lambda step: device(x, y, z_at(step), core)
    to_y = lambda step: device(x, y_peers[step % NY], z, core)
    gather_az = Gather(NZ, z, to_z, lambda i: rows_a.at[i], half_rows, az_send, az_recv)
    gather_bz = Gather(NZ, z, to_z, lambda i: rows_b.at[y, i], half_columns, bz_send, bz_recv)
    gather_by = Gather(NY, y, to_y, lambda i: rows_b.at[i], half_rows, by_send, by_recv)
    gather_bz.send(0)
    share_far(0)
    send_far(2)
    for j in range(1, NY):
        place = rows_a.at[z, y_peers[NY - j]]
        send_to(
            place, place, ay_send.at[j], ay_recv.at[j], device(x, y_peers[j], z, core)
        ).wait_recv()
    gather_az.send(0)
    gather_bz.wait(0)
    gather_bz.send(1)
    gather_bz.wait(1)
    gather_bz.send(2)
    gather_az.wait(0)
    gather_az.send(1)
    gather_bz.wait(2)
    gather_bz.send(3)
    gather_bz.wait(3)
    gather_by.send(0)
    share_far(1)
    gather_az.wait(1)
    gather_az.send(2)
    share_far(2)
    for number in range(3):
        settle(number)

    first_expert = 2 * (z * NY + y)

    def compute(rows, out, places):
        lead = rows.shape[1] * rows.shape[2]
        count = lead * len(places)
        block = jnp.concatenate([rows[i].reshape(lead, AUG) for i in places], axis=0)
        inputs = block[:, 0:WIDTH]
        gates = block[:, WIDTH:AUG].astype(F32)
        number = lax.rem(lax.broadcasted_iota(jnp.int32, (count, 128), 1), 64)
        answer = None
        for e in range(2):
            gate = jnp.sum(
                jnp.where(number == first_expert + e, gates, 0.0), axis=1, keepdims=True
            )
            gate_act = jnp.dot(inputs, wg[e], preferred_element_type=F32)
            up_act = jnp.dot(inputs, wu[e], preferred_element_type=F32)
            hidden = (gate_act / (1.0 + jnp.exp(-gate_act)) * up_act * gate).astype(BF16)
            term = jnp.dot(hidden, wd[e], preferred_element_type=F32)
            answer = term if answer is None else answer + term
        for at, i in enumerate(places):
            out[i] = answer[at * lead : (at + 1) * lead].reshape(
                rows.shape[1], rows.shape[2], WIDTH
            )

    scatter_az = Scatter(
        NZ, z, to_z, lambda i: out_a.at[i], half_rows, stage_az, came_az, raz_send, raz_recv
    )
    scatter_by = Scatter(
        NY, y, to_y, lambda i: out_b.at[i], half_rows, stage_by, came_by, rby_send, rby_recv
    )
    scatter_bz = Scatter(
        NZ, z, to_z, lambda i: sum_b.at[i], half_columns, stage_bz, came_bz, rbz_send, rbz_recv
    )
    compute(rows_a, out_a, [z, z_at(1), z_at(-1), z_at(2)])
    gather_az.wait(2)
    gather_az.send(3)
    gather_by.wait(0)
    gather_by.send(1)
    compute(rows_b, out_b, [y, y_peers[1]])
    gather_az.wait(3)
    compute(rows_a, out_a, [z_at(4), z_at(3), z_at(-3), z_at(-2)])
    scatter_az.send(0)
    gather_by.wait(1)
    compute(rows_b, out_b, [y_peers[2], y_peers[3]])
    scatter_by.send(0)
    scatter_az.send(1)
    scatter_by.send(1)
    scatter_az.send(2)
    scatter_az.send(3)
    sum_b[...] = scatter_by.result()
    scatter_bz.send(0)
    sum_a[...] = scatter_az.result()
    stage_ay[...] = sum_a[...].astype(BF16)
    for j in range(1, NY):
        copy = send_to(
            stage_ay.at[y_peers[j]],
            came_ay.at[y],
            ry_send.at[j],
            ry_recv.at[j],
            device(x, y_peers[j], z, core),
        )
        copy.start()
        sent.append(copy)
    scatter_bz.send(1)
    scatter_bz.send(2)
    scatter_bz.send(3)
    upper = sum_a[y]
    for j in range(1, NY):
        send_to(
            stage_ay.at[y_peers[j]],
            came_ay.at[y_peers[NY - j]],
            ry_send.at[j],
            ry_recv.at[j],
            device(x, y_peers[j], z, core),
        ).wait_recv()
        upper = upper + came_ay[y_peers[NY - j]].astype(F32)
    lower = scatter_bz.result()
    answer = resid[...].astype(F32) + jnp.concatenate([upper, lower], axis=0)
    answer = answer.astype(BF16)
    for j in range(NX):
        mixed[j] = answer[:, j * COLS : (j + 1) * COLS]
    for j in range(1, NX):
        copy = send_to(
            mixed.at[peers[j]],
            came_x.at[x],
            x_send.at[j],
            x_recv.at[j],
            device(peers[j], y, z, core),
        )
        copy.start()
        sent.append(copy)
    out_ref[pl.ds(pl.multiple_of(x * QUARTER, QUARTER), QUARTER), :] = mixed[x]
    for j in range(1, NX):
        source = peers[NX - j]
        send_to(
            mixed.at[peers[j]],
            came_x.at[source],
            x_send.at[j],
            x_recv.at[j],
            device(peers[j], y, z, core),
        ).wait_recv()
        out_ref[pl.ds(pl.multiple_of(source * QUARTER, QUARTER), QUARTER), :] = came_x[source]
    for copy in sent:
        copy.wait_send()
    for ring in (
        gather_az,
        gather_bz,
        gather_by,
        scatter_az,
        scatter_by,
        scatter_bz,
    ):
        for copy in ring.sent:
            copy.wait_send()


def shards(
    tokens,
    attn_gain,
    q_weight,
    key_matrix,
    value_matrix,
    o_weight,
    moe_gain,
    gate_weight,
    up_weight,
    down_weight,
    key_page_pool,
    value_page_pool,
    cache_lens,
    page_table,
    routes,
    route_gates,
):
    vmem = pl.BlockSpec(memory_space=pltpu.VMEM)
    smem = pl.BlockSpec(memory_space=pltpu.SMEM)
    hbm = pl.BlockSpec(memory_space=pl.ANY)
    dma = pltpu.SemaphoreType.DMA
    length = cache_lens[0]
    places = (length + jnp.arange(ROWS, dtype=jnp.int32)).astype(F32)
    entry = jnp.arange(128, dtype=jnp.int32) % HEAD
    frequency = 10000.0 ** (-2.0 * (entry % (HEAD // 2)).astype(F32) / HEAD)
    angle = places[:, None] * frequency
    cosine = jnp.cos(angle)
    sine = jnp.where(entry < HEAD // 2, -1.0, 1.0) * jnp.sin(angle)
    shape = jax.ShapeDtypeStruct
    pair = lambda *dims: pltpu.VMEM((2, *dims), BF16)
    both = lambda *dims: [dma(dims), dma(dims)]
    return pl.pallas_call(
        layer_kernel,
        out_shape=shape((ROWS, COLS), BF16),
        in_specs=[smem] + [vmem] * 8 + [hbm] * 9,
        out_specs=vmem,
        scratch_shapes=[
            pltpu.VMEM((NX, ROWS, COLS), BF16),
            pltpu.VMEM((WIDTH, COLS), BF16),
            pltpu.VMEM((WIDTH, 128), BF16),
            pltpu.VMEM((WIDTH, 128), BF16),
            pltpu.VMEM((COLS, WIDTH), BF16),
            pltpu.VMEM((CACHE, 256), BF16),
            pltpu.VMEM((CACHE, 128), BF16),
            pltpu.VMEM((STACK, 256), BF16),
            pltpu.VMEM((STACK, 1), F32),
            pltpu.VMEM((STACK, 1), F32),
            pltpu.VMEM((STACK, 128), F32),
            pltpu.VMEM((NX, QUARTER, WIDTH), BF16),
            pltpu.VMEM((NX, QUARTER, WIDTH), BF16),
            pltpu.VMEM((NX, QUARTER, WIDTH), F32),
            pltpu.VMEM((ROWS, 128), F32),
            pltpu.VMEM((QUARTER, WIDTH), BF16),
            pltpu.VMEM((NZ, NY, HALF, AUG), BF16),
            pltpu.VMEM((NY, NZ, HALF, AUG), BF16),
            pair(WIDTH, FFE),
            pair(WIDTH, FFE),
            pair(FFE, WIDTH),
            pltpu.VMEM((NZ, NY, HALF, WIDTH), F32),
            pltpu.VMEM((NY, NZ, HALF, WIDTH), F32),
            pltpu.VMEM((NY, HALF, WIDTH), F32),
            pltpu.VMEM((NZ, HALF, WIDTH), F32),
            pair(NZ // 2, NY, HALF, WIDTH),
            pair(NZ // 2, NY, HALF, WIDTH),
            pltpu.VMEM((NY, HALF, WIDTH), BF16),
            pltpu.VMEM((NY, HALF, WIDTH), BF16),
            pair(NY // 2, NZ, HALF, WIDTH),
            pair(NY // 2, NZ, HALF, WIDTH),
            pair(NZ // 2, HALF, WIDTH),
            pair(NZ // 2, HALF, WIDTH),
            pltpu.VMEM((NX, QUARTER, COLS), BF16),
            pltpu.VMEM((NX, QUARTER, COLS), BF16),
            dma((4,)),
            dma((BLOCKS,)),
            dma((BLOCKS,)),
            *both(NX),
            *both(NX),
            dma((3,)),
            *both(3, 2),
            *both(3, 2),
            *both(3, NX),
            *both(NY),
            *both(2, NZ // 2),
            *both(2, NY // 2),
            *both(2, NZ // 2),
            *both(NY),
            *both(2, NZ // 2),
            *both(2, NY // 2),
            *both(2, NZ // 2),
            *both(NX),
        ],
        compiler_params=pltpu.CompilerParams(
            collective_id=0, has_side_effects=True, vmem_limit_bytes=62 << 20
        ),
        name="layer",
    )(
        cache_lens,
        page_table,
        tokens,
        cosine,
        sine,
        routes.T,
        route_gates.T,
        attn_gain,
        moe_gain,
        q_weight,
        key_matrix,
        value_matrix,
        o_weight,
        key_page_pool.reshape(CACHE, 128),
        value_page_pool.reshape(CACHE, 128),
        gate_weight[0],
        up_weight[0],
        down_weight[0],
    )


def solution(mesh):
    in_specs = (
        P("seq", "tensor"),
        P(),
        P(None, "tensor"),
        P(None, "tensor"),
        P(None, "tensor"),
        P("tensor", None),
        P(),
        P("seq", None, "tensor"),
        P("seq", None, "tensor"),
        P("seq", "tensor", None),
        P("seq", None, "tensor"),
        P("seq", None, "tensor"),
        P("seq"),
        P("seq", None),
        P("seq", None),
        P("seq", None),
    )
    out_specs = P("seq", "tensor")
    return jax.shard_map(shards, mesh=mesh, in_specs=in_specs, out_specs=out_specs, check_vma=False)
```

time: 137 us -> 131 us (0.956)
  local copies, waits for them, and re-layouts: 7.76 us -> 1.54 us
  Pallas kernels: 125 us -> 127 us
  other arithmetic: 2.39 us -> 0.98 us
    unnamed x3 -> x1, local copies, waits for them, and re-layouts: 4.36 us -> 1.54 us
    reshape x2 -> x0, local copies, waits for them, and re-layouts: 2.6 us -> none  [the longest x1 1.3 us: shards(): moe_gain.reshape(1, WIDTH)]
    pallas_call x2 -> x1, Pallas kernels: 125 us -> 127 us  [shards(): pl.pallas_call(layer_kernel, out_shape=shape((ROWS, COLS), BF16), in_spec...]
where the time goes in v2:
time: 131 us; the launch traced here: 130 us
  Pallas kernels  127 us (97%)
  local copies, waits for them, and re-layouts  1.54 us (1%)
    pallas_call x1, Pallas kernels, shards(): pl.pallas_call(layer_kernel, out_shape=shape((ROWS, COLS), BF16), in_spec...  127 us

profile of v2, /device:TPU:8, one launch (start us, length us, event | category | flops | bytes accessed | tf_op | source)
XLA Modules:
  0.0 130.4 jit_solution(1404980241603364233)
XLA Ops:
  0.7 1.0 fusion
  1.6 127.2 %layer.1 = bf16[128,384]{1,0:T(8,128)(2,1)} custom-call(s32[1]{0:T(128)} %copy.18.length_ref, s32[1,64]{1,0:T(1,128)} %table_ref.1, bf16[128,384]{1,0:T(8,128)(2,1)} %tokens_ref.1, f32[128,128]{1,0:T(8,128)} %get-tuple-element.6.cos_ref, f32[128,128]{1,0:T(8,128)} %get-tuple-element.5.sin_ref, s32[8,128]{1,0:T(8,128)} %bitcast.14, f32[8,128]{1,0:T(8,128)} %bitcast.15, ...), custom_call_target="tpu_custom_call" | custom-call | tf_op jit(solution)/shard_map/layer/pallas_call | solution.py:730
  128.9 1.5 %copy.19 = bf16[128,384]{1,0:T(8,128)(2,1)} copy(bf16[128,384]{1,0:T(8,128)(2,1)} %layer.1) | data formatting | bytes 196608
  (2 shorter events, 0.0 us)

commit v3 on v2

--- a/solution.py
+++ b/solution.py
@@ -76,92 +76,104 @@
 
 
 class Gather:
-    def __init__(self, size, me, target, place, halves, send_sem, recv_sem):
+    def __init__(self, size, me, target, place, parts, send_sem, recv_sem):
         self.size, self.me, self.target = size, me, target
-        self.place, self.halves = place, halves
+        self.place, self.parts = place, parts
         self.send_sem, self.recv_sem = send_sem, recv_sem
         self.sent = []
 
-    def copies(self, k, arriving):
+    def copies(self, k, s, arriving):
         last = k + 1 == self.size // 2
         made = []
         for way in range(2):
+            if last and self.parts > 1 and s // (self.parts // 2) != way:
+                continue
             if arriving:
                 shift = -(1 + k) if way == 0 else 1 + k
             else:
                 shift = -k if way == 0 else k
-            ref = self.place(lax.rem(self.me + shift + self.size, self.size))
-            if last:
-                ref = self.halves(ref)[way]
+            ref = self.place(lax.rem(self.me + shift + self.size, self.size), s)
+            if last and self.parts == 1:
+                ref = half_columns(ref)[way]
             made.append(
                 send_to(
                     ref,
                     ref,
-                    self.send_sem.at[way, k],
-                    self.recv_sem.at[way, k],
+                    self.send_sem.at[way, k, s],
+                    self.recv_sem.at[way, k, s],
                     self.target(1 if way == 0 else -1),
                 )
             )
         return made
 
-    def send(self, k):
-        for copy in self.copies(k, False):
+    def send(self, k, s=0):
+        for copy in self.copies(k, s, False):
             copy.start()
             self.sent.append(copy)
 
-    def wait(self, k):
-        for copy in self.copies(k, True):
+    def wait(self, k, s=0):
+        for copy in self.copies(k, s, True):
             copy.wait_recv()
 
+    def relay(self, k, *parts):
+        for s in parts:
+            self.wait(k, s)
+            self.send(k + 1, s)
+
 
 class Scatter:
-    def __init__(self, size, me, target, own, halves, stage, arrived, send_sem, recv_sem):
+    def __init__(self, size, me, target, own, parts, stage, arrived, send_sem, recv_sem):
         self.size, self.me, self.target = size, me, target
-        self.own, self.halves = own, halves
+        self.own, self.parts = own, parts
         self.stage, self.arrived = stage, arrived
         self.send_sem, self.recv_sem = send_sem, recv_sem
         self.sent = []
 
-    def copy(self, way, k):
-        src, dst = self.stage.at[way, k], self.arrived.at[way, k]
-        if k == 0:
-            src, dst = self.halves(src)[way], self.halves(dst)[way]
+    def copy(self, way, k, s):
+        src, dst = self.stage.at[way, k, s], self.arrived.at[way, k, s]
+        if k == 0 and self.parts == 1:
+            src, dst = half_columns(src)[way], half_columns(dst)[way]
         return send_to(
             src,
             dst,
-            self.send_sem.at[way, k],
-            self.recv_sem.at[way, k],
+            self.send_sem.at[way, k, s],
+            self.recv_sem.at[way, k, s],
             self.target(1 if way == 0 else -1),
         )
 
-    def send(self, k):
+    def send(self, k, s=0):
         distance = self.size // 2 - k
         for way in range(2):
+            mine = self.parts == 1 or s // (self.parts // 2) == way
+            if k == 0 and not mine:
+                continue
             shift = distance if way == 0 else -distance
-            own = self.own(lax.rem(self.me + shift + self.size, self.size))
-            here = self.stage.at[way, k]
-            if k == 0:
-                self.halves(here)[way][...] = self.halves(own)[way][...].astype(BF16)
-            elif k == 1:
-                self.copy(way, 0).wait_recv()
-                came = self.halves(self.arrived.at[way, 0])[way]
-                self.halves(here)[way][...] = (
-                    self.halves(own)[way][...] + came[...].astype(F32)
+            own = self.own(lax.rem(self.me + shift + self.size, self.size), s)
+            here = self.stage.at[way, k, s]
+            if k == 0 and self.parts == 1:
+                half_columns(here)[way][...] = half_columns(own)[way][...].astype(BF16)
+            elif k == 0 or (k == 1 and not mine):
+                here[...] = own[...].astype(BF16)
+            elif k == 1 and self.parts == 1:
+                self.copy(way, 0, s).wait_recv()
+                came = half_columns(self.arrived.at[way, 0, s])[way]
+                half_columns(here)[way][...] = (
+                    half_columns(own)[way][...] + came[...].astype(F32)
                 ).astype(BF16)
-                self.halves(here)[1 - way][...] = self.halves(own)[1 - way][...].astype(BF16)
+                half_columns(here)[1 - way][...] = half_columns(own)[1 - way][...].astype(BF16)
             else:
-                self.copy(way, k - 1).wait_recv()
-                here[...] = (own[...] + self.arrived[way, k - 1].astype(F32)).astype(BF16)
-            copy = self.copy(way, k)
+                self.copy(way, k - 1, s).wait_recv()
+                here[...] = (own[...] + self.arrived[way, k - 1, s].astype(F32)).astype(BF16)
+            copy = self.copy(way, k, s)
             copy.start()
             self.sent.append(copy)
 
-    def result(self):
+    def result(self, s=0):
         k = self.size // 2 - 1
-        answer = self.own(self.me)[...]
+        answer = self.own(self.me, s)[...]
         for way in range(2):
-            self.copy(way, k).wait_recv()
-            answer = answer + self.arrived[way, k].astype(F32)
+            self.copy(way, k, s).wait_recv()
+            answer = answer + self.arrived[way, k, s].astype(F32)
         return answer
 
 
@@ -173,11 +185,6 @@
         ref.at[(*lead, pl.ds(0, split))],
         ref.at[(*lead, pl.ds(split, width - split))],
     )
-
-
-def half_rows(ref):
-    size = ref.shape[0] // 2
-    return ref.at[pl.ds(0, size)], ref.at[pl.ds(size, size)]
 
 
 def layer_kernel(
@@ -223,7 +230,6 @@
     wd,
     out_a,
     out_b,
-    sum_a,
     sum_b,
     stage_az,
     came_az,
@@ -538,7 +544,7 @@
     rows_a[z, y] = augmented[0:HALF]
     rows_b[y, z] = augmented[HALF:QUARTER]
 
-    for j in range(1, NY):
+    for j in (1, 3, 2):
         begin(
             send_to(
                 rows_a.at[z, y],
@@ -550,31 +556,52 @@
         )
     to_z = lambda step: device(x, y, z_at(step), core)
     to_y = lambda step: device(x, y_peers[step % NY], z, core)
-    gather_az = Gather(NZ, z, to_z, lambda i: rows_a.at[i], half_rows, az_send, az_recv)
-    gather_bz = Gather(NZ, z, to_z, lambda i: rows_b.at[y, i], half_columns, bz_send, bz_recv)
-    gather_by = Gather(NY, y, to_y, lambda i: rows_b.at[i], half_rows, by_send, by_recv)
+    near_y = (0, 1, 3, 2)
+    near_z = (0, 1, -1, 2, -2, 3, -3, 4)
+    gather_az = Gather(
+        NZ, z, to_z, lambda i, s: rows_a.at[i, y_peers[near_y[s]]], NY, az_send, az_recv
+    )
+    gather_bz = Gather(NZ, z, to_z, lambda i, s: rows_b.at[y, i], 1, bz_send, bz_recv)
+    gather_by = Gather(
+        NY, y, to_y, lambda i, s: rows_b.at[i, z_at(near_z[s])], NZ, by_send, by_recv
+    )
     gather_bz.send(0)
-    share_far(0)
-    send_far(2)
-    for j in range(1, NY):
-        place = rows_a.at[z, y_peers[NY - j]]
+    gather_by.send(0, 0)
+    gather_az.send(0, 0)
+
+    def take_y(s):
+        j = NY - near_y[s]
+        place = rows_a.at[z, y_peers[near_y[s]]]
         send_to(
             place, place, ay_send.at[j], ay_recv.at[j], device(x, y_peers[j], z, core)
         ).wait_recv()
-    gather_az.send(0)
-    gather_bz.wait(0)
-    gather_bz.send(1)
-    gather_bz.wait(1)
-    gather_bz.send(2)
-    gather_az.wait(0)
-    gather_az.send(1)
-    gather_bz.wait(2)
-    gather_bz.send(3)
+        gather_az.send(0, s)
+
+    share_far(0)
+    send_far(2)
+    gather_bz.relay(0, 0)
+    gather_by.send(0, 1)
+    gather_by.send(0, 2)
+    for s in range(1, NY):
+        take_y(s)
+    gather_az.relay(0, 0)
+    gather_bz.relay(1, 0)
+    gather_by.send(0, 3)
+    gather_by.send(0, 4)
+    gather_by.relay(0, 0)
+    gather_az.relay(0, 1)
+    gather_bz.relay(2, 0)
+    gather_by.send(0, 5)
+    gather_by.send(0, 6)
+    gather_az.relay(0, 2, 3)
+    gather_by.relay(0, 1, 2)
     gather_bz.wait(3)
-    gather_by.send(0)
+    gather_by.send(0, 7)
+    gather_az.relay(1, 0, 1)
+    gather_by.relay(0, 3)
+    gather_az.relay(1, 2, 3)
+    gather_by.relay(0, 4)
     share_far(1)
-    gather_az.wait(1)
-    gather_az.send(2)
     share_far(2)
     for number in range(3):
         settle(number)
@@ -603,49 +630,90 @@
                 rows.shape[1], rows.shape[2], WIDTH
             )
 
+    far_y = (2, 1, 3, 0)
+    far_z = (4, 3, -3, 2, -2, 1, -1, 0)
     scatter_az = Scatter(
-        NZ, z, to_z, lambda i: out_a.at[i], half_rows, stage_az, came_az, raz_send, raz_recv
+        NZ,
+        z,
+        to_z,
+        lambda i, s: out_a.at[i, y_peers[far_y[s]]],
+        NY,
+        stage_az,
+        came_az,
+        raz_send,
+        raz_recv,
     )
     scatter_by = Scatter(
-        NY, y, to_y, lambda i: out_b.at[i], half_rows, stage_by, came_by, rby_send, rby_recv
+        NY,
+        y,
+        to_y,
+        lambda i, s: out_b.at[i, z_at(far_z[s])],
+        NZ,
+        stage_by,
+        came_by,
+        rby_send,
+        rby_recv,
     )
     scatter_bz = Scatter(
-        NZ, z, to_z, lambda i: sum_b.at[i], half_columns, stage_bz, came_bz, rbz_send, rbz_recv
+        NZ, z, to_z, lambda i, s: sum_b.at[i], 1, stage_bz, came_bz, rbz_send, rbz_recv
     )
     compute(rows_a, out_a, [z, z_at(1), z_at(-1), z_at(2)])
-    gather_az.wait(2)
-    gather_az.send(3)
-    gather_by.wait(0)
-    gather_by.send(1)
+    gather_az.relay(2, 0, 1)
+    gather_by.relay(0, 5, 6)
+    gather_az.relay(2, 2, 3)
+    gather_by.relay(0, 7)
     compute(rows_b, out_b, [y, y_peers[1]])
-    gather_az.wait(3)
+    for s in range(NY):
+        gather_az.wait(3, s)
     compute(rows_a, out_a, [z_at(4), z_at(3), z_at(-3), z_at(-2)])
-    scatter_az.send(0)
-    gather_by.wait(1)
+    for s in range(NY):
+        scatter_az.send(0, s)
+    for s in range(NZ):
+        gather_by.wait(1, s)
     compute(rows_b, out_b, [y_peers[2], y_peers[3]])
-    scatter_by.send(0)
-    scatter_az.send(1)
-    scatter_by.send(1)
-    scatter_az.send(2)
-    scatter_az.send(3)
-    sum_b[...] = scatter_by.result()
+    for s in range(NZ):
+        scatter_by.send(0, s)
+    for s in range(NY):
+        scatter_az.send(1, s)
+    for s in range(NZ):
+        scatter_by.send(1, s)
+        if s % 2:
+            scatter_az.send(2, s // 2)
+
+    def take_b(*parts):
+        for s in parts:
+            sum_b[z_at(far_z[s])] = scatter_by.result(s)
+
+    def give_y(s):
+        j = far_y[s]
+        stage_ay[y_peers[j]] = scatter_az.result(s).astype(BF16)
+        begin(
+            send_to(
+                stage_ay.at[y_peers[j]],
+                came_ay.at[y],
+                ry_send.at[j],
+                ry_recv.at[j],
+                device(x, y_peers[j], z, core),
+            )
+        )
+
+    take_b(0)
     scatter_bz.send(0)
-    sum_a[...] = scatter_az.result()
-    stage_ay[...] = sum_a[...].astype(BF16)
-    for j in range(1, NY):
-        copy = send_to(
-            stage_ay.at[y_peers[j]],
-            came_ay.at[y],
-            ry_send.at[j],
-            ry_recv.at[j],
-            device(x, y_peers[j], z, core),
-        )
-        copy.start()
-        sent.append(copy)
+    scatter_az.send(3, 0)
+    scatter_az.send(3, 1)
+    take_b(1, 2)
     scatter_bz.send(1)
+    scatter_az.send(3, 2)
+    scatter_az.send(3, 3)
+    take_b(3, 4)
     scatter_bz.send(2)
+    give_y(0)
+    take_b(5, 6)
     scatter_bz.send(3)
-    upper = sum_a[y]
+    give_y(1)
+    give_y(2)
+    upper = scatter_az.result(3)
+    take_b(7)
     for j in range(1, NY):
         send_to(
             stage_ay.at[y_peers[j]],
@@ -756,7 +824,6 @@
             pair(FFE, WIDTH),
             pltpu.VMEM((NZ, NY, HALF, WIDTH), F32),
             pltpu.VMEM((NY, NZ, HALF, WIDTH), F32),
-            pltpu.VMEM((NY, HALF, WIDTH), F32),
             pltpu.VMEM((NZ, HALF, WIDTH), F32),
             pair(NZ // 2, NY, HALF, WIDTH),
             pair(NZ // 2, NY, HALF, WIDTH),
@@ -764,8 +831,8 @@
             pltpu.VMEM((NY, HALF, WIDTH), BF16),
             pair(NY // 2, NZ, HALF, WIDTH),
             pair(NY // 2, NZ, HALF, WIDTH),
-            pair(NZ // 2, HALF, WIDTH),
-            pair(NZ // 2, HALF, WIDTH),
+            pair(NZ // 2, 1, HALF, WIDTH),
+            pair(NZ // 2, 1, HALF, WIDTH),
             pltpu.VMEM((NX, QUARTER, COLS), BF16),
             pltpu.VMEM((NX, QUARTER, COLS), BF16),
             dma((4,)),
@@ -778,13 +845,13 @@
             *both(3, 2),
             *both(3, NX),
             *both(NY),
-            *both(2, NZ // 2),
-            *both(2, NY // 2),
-            *both(2, NZ // 2),
+            *both(2, NZ // 2, NY),
+            *both(2, NY // 2, NZ),
+            *both(2, NZ // 2, 1),
             *both(NY),
-            *both(2, NZ // 2),
-            *both(2, NY // 2),
-            *both(2, NZ // 2),
+            *both(2, NZ // 2, NY),
+            *both(2, NY // 2, NZ),
+            *both(2, NZ // 2, 1),
             *both(NX),
         ],
         compiler_params=pltpu.CompilerParams(

time: 131 us -> 120 us (0.916)
  Pallas kernels: 127 us -> 116 us
    pallas_call x1, Pallas kernels: 127 us -> 116 us  [shards(): pl.pallas_call(layer_kernel, out_shape=shape((ROWS, COLS), BF16), in_spec...]
where the time goes in v3:
time: 120 us
  Pallas kernels  116 us (97%)
  local copies, waits for them, and re-layouts  1.54 us (1%)
    pallas_call x1, Pallas kernels, shards(): pl.pallas_call(layer_kernel, out_shape=shape((ROWS, COLS), BF16), in_spec...  116 us

profile of v3, /device:TPU:8, one launch (start us, length us, event | category | flops | bytes accessed | tf_op | source)
XLA Modules:
  0.0 119.6 jit_solution(13209123940379375999)
XLA Ops:
  0.7 1.0 fusion
  1.6 116.4 %layer.1 = bf16[128,384]{1,0:T(8,128)(2,1)} custom-call(s32[1]{0:T(128)} %copy.18.length_ref, s32[1,64]{1,0:T(1,128)} %table_ref.1, bf16[128,384]{1,0:T(8,128)(2,1)} %tokens_ref.1, f32[128,128]{1,0:T(8,128)} %get-tuple-element.6.cos_ref, f32[128,128]{1,0:T(8,128)} %get-tuple-element.5.sin_ref, s32[8,128]{1,0:T(8,128)} %bitcast.14, f32[8,128]{1,0:T(8,128)} %bitcast.15, ...), custom_call_target="tpu_custom_call" | custom-call | tf_op jit(solution)/shard_map/layer/pallas_call | solution.py:798
  118.1 1.5 %copy.19 = bf16[128,384]{1,0:T(8,128)(2,1)} copy(bf16[128,384]{1,0:T(8,128)(2,1)} %layer.1) | data formatting | bytes 196608
  (2 shorter events, 0.0 us)

commit v4 on v3

--- a/solution.py
+++ b/solution.py
@@ -494,7 +494,6 @@
 
     lax.fori_loop(0, 4, step, 0)
     send_far(0)
-    send_near(2)
     lax.fori_loop(4, 7, step, 0)
     send_far(1)
     lax.fori_loop(7, BLOCKS, step, 0)
@@ -524,6 +523,8 @@
         copy.start()
         sent.append(copy)
 
+    send_near(2)
+
     my_rows = pl.ds(pl.multiple_of(x * QUARTER, QUARTER), QUARTER)
     residual = partial[x] + jnp.concatenate(
         [tok[j, my_rows, :].astype(F32) for j in range(NX)], axis=1
@@ -578,7 +579,6 @@
         gather_az.send(0, s)
 
     share_far(0)
-    send_far(2)
     gather_bz.relay(0, 0)
     gather_by.send(0, 1)
     gather_by.send(0, 2)
@@ -594,6 +594,7 @@
     gather_by.send(0, 5)
     gather_by.send(0, 6)
     gather_az.relay(0, 2, 3)
+    send_far(2)
     gather_by.relay(0, 1, 2)
     gather_bz.wait(3)
     gather_by.send(0, 7)

time: 120 us -> 116 us (0.967)
  Pallas kernels: 116 us -> 113 us
    pallas_call x1, Pallas kernels: 116 us -> 113 us  [shards(): pl.pallas_call(layer_kernel, out_shape=shape((ROWS, COLS), BF16), in_spec...]
where the time goes in v4:
time: 116 us
  Pallas kernels  113 us (97%)
  local copies, waits for them, and re-layouts  1.54 us (1%)
    pallas_call x1, Pallas kernels, shards(): pl.pallas_call(layer_kernel, out_shape=shape((ROWS, COLS), BF16), in_spec...  113 us

profile of v4, /device:TPU:8, one launch (start us, length us, event | category | flops | bytes accessed | tf_op | source)
XLA Modules:
  0.0 115.9 jit_solution(18048856745391209322)
XLA Ops:
  0.7 1.0 fusion
  1.6 112.7 %layer.1 = bf16[128,384]{1,0:T(8,128)(2,1)} custom-call(s32[1]{0:T(128)} %copy.18.length_ref, s32[1,64]{1,0:T(1,128)} %table_ref.1, bf16[128,384]{1,0:T(8,128)(2,1)} %tokens_ref.1, f32[128,128]{1,0:T(8,128)} %get-tuple-element.6.cos_ref, f32[128,128]{1,0:T(8,128)} %get-tuple-element.5.sin_ref, s32[8,128]{1,0:T(8,128)} %bitcast.14, f32[8,128]{1,0:T(8,128)} %bitcast.15, ...), custom_call_target="tpu_custom_call" | custom-call | tf_op jit(solution)/shard_map/layer/pallas_call | solution.py:799
  114.4 1.5 %copy.19 = bf16[128,384]{1,0:T(8,128)(2,1)} copy(bf16[128,384]{1,0:T(8,128)(2,1)} %layer.1) | data formatting | bytes 196608
  (2 shorter events, 0.0 us)
